TPU v7x, 32 devices: a whole 2x2x4 slice. The times are simulated.
32 devices in a mesh: pat: 8 (over y, x, core), code: 4 (over z).
Axes of the slice: x: 2, y: 2, z: 4, core: 2. Of those that a mesh axis runs over, the one named last changes fastest.
Arguments:
- tile_data: bfloat16 [8, 4, 16, 128, 512], P('pat', 'code'), may hold values from 0 to 7, as said below
- tile_list: int32 [8, 4, 3, 16], P('pat', 'code'), may hold values from 0 to 31, as said below
- tile_count: int32 [8, 4], P('pat', 'code'), may hold values from 8 to 16, as said below
- visit_counts: int32 [128], P('pat'), may hold values from 1 to 256, as said below
- code_factor_t: float32 [64, 65536], P(None, 'code'), may hold values from 0.004 to 0.33, as said below
- visit_mix: float32 [64, 64], replicated, may hold values from -0.15 to 1.2
- patient_weight: float32 [128, 64], P('pat'), may hold values from 0.5 to 30, as said below
Outputs:
- code_factor_new: float32 [64, 65536], P(None, 'code')
- mix_new: float32 [64, 64], replicated
- patient_weight_new: float32 [128, 64], P(('pat', 'code'))
Inputs may be any that keep to these rules, and one draw needn't show every extreme that they name: `tile_list`: for device (p, c) and slot t: entry 0 is a patient of pat index p (0 to 15), entry 1 a visit block below that patient's visits divided by 128 and rounded up, entry 2 a code block of code index c (0 to 31). A triple may repeat; such tiles add. `tile_count`: slots at or past a device's count are not in use; some device uses all slots. `visit_counts`: some patient has 256 visits. `tile_data`: Whole-number counts. Rows past the patient's visit count and slots not in use hold left-over values that are not part of the data. `code_factor_t`: Positive. `patient_weight`: Positive.
All inputs are finite; a program needn't handle non-finite values.
Results may differ from a plain program's by a relative error of at most 0.0073.
Values may be sent and summed in bfloat16 or wider, within the bound.
A program may use at most 64 MiB of HBM per device.

v0:
```python
import functools

import jax
import jax.numpy as jnp
from jax import lax
from jax.experimental import pallas as pl
from jax.experimental.pallas import tpu as pltpu
from jax.sharding import PartitionSpec as P

VBLOCKS = 2
NS_STEPS = 8
MESH = pl.DeviceIdType.MESH
damping = 0.1
epsilon = 1e-06

f32 = jnp.float32
bf16 = jnp.bfloat16
VMEM = pl.BlockSpec(memory_space=pltpu.VMEM)
SMEM = pl.BlockSpec(memory_space=pltpu.SMEM)
LIMIT = 60 * 1024 * 1024


def mm(left, right, left_dim=1, right_dim=0):
    return lax.dot_general(
        left,
        right,
        (((left_dim,), (right_dim,)), ((), ())),
        precision=lax.Precision.HIGHEST,
        preferred_element_type=f32,
    )


def bmm(left, right, left_dim=1, right_dim=0):
    return lax.dot_general(
        left, right, (((left_dim,), (right_dim,)), ((), ())), preferred_element_type=f32
    )


def damped_inverse(gram):
    size = gram.shape[0]
    row_at = lax.broadcasted_iota(jnp.int32, (size, size), 0)
    lane_at = lax.broadcasted_iota(jnp.int32, (size, size), 1)
    lane_one = lax.broadcasted_iota(jnp.int32, (1, size), 1)
    on_diag = row_at == lane_at
    trace = jnp.sum(jnp.sum(jnp.where(on_diag, gram, 0.0), axis=1, keepdims=True), axis=0, keepdims=True)
    a = gram + jnp.where(on_diag, trace * (damping / size), 0.0)
    for k in range(0, size, 2):
        row_p, row_q = a[k : k + 1, :], a[k + 1 : k + 2, :]
        col_p, col_q = a[:, k : k + 1], a[:, k + 1 : k + 2]
        pp, pq, qq = a[k : k + 1, k : k + 1], a[k : k + 1, k + 1 : k + 2], a[k + 1 : k + 2, k + 1 : k + 2]
        scale = 1.0 / (pp * qq - pq * pq)
        at_p, at_q = lane_one == k, lane_one == k + 1
        row_p = jnp.where(at_p, 1.0, jnp.where(at_q, 0.0, row_p))
        row_q = jnp.where(at_q, 1.0, jnp.where(at_p, 0.0, row_q))
        new_p = (qq * scale) * row_p - (pq * scale) * row_q
        new_q = (pp * scale) * row_q - (pq * scale) * row_p
        kept = jnp.where((lane_at == k) | (lane_at == k + 1), 0.0, a)
        a = kept - col_p * new_p - col_q * new_q
        a = jnp.where(row_at == k, new_p, jnp.where(row_at == k + 1, new_q, a))
    return a


def live_rows(list_ref, count_ref, visits_ref, slot, tile_rows):
    owner, block, code = list_ref[0, slot], list_ref[1, slot], list_ref[2, slot]
    limit = jnp.where(slot < count_ref[0], visits_ref[owner] - block * tile_rows, 0)
    return owner * VBLOCKS + block, code, limit


def products_kernel(list_ref, count_ref, visits_ref, tiles, factor, dev, col, gram, split, acc):
    slots, tile_rows, tile_cols = tiles.shape
    rank, codes = factor.shape
    step = min(2048, codes)
    total = jnp.zeros((2 * rank, 2 * rank), f32)
    profile = jnp.zeros((rank, 1), f32)
    for start in range(0, codes, step):
        part = factor[:, start : start + step]
        high = part.astype(bf16)
        split[:rank, start : start + step] = high
        split[rank:, start : start + step] = (part - high.astype(f32)).astype(bf16)
        profile += jnp.sum(part, axis=1, keepdims=True)
        both = split[:, start : start + step]
        total += bmm(both, both, 1, 1)
    profile = profile * (1.0 / codes)
    square = total[:rank, :rank] + total[:rank, rank:] + total[rank:, :rank] + total[rank:, rank:]
    both = jnp.concatenate([square, jnp.broadcast_to(profile, (rank, rank))], axis=1)
    rows = gram.shape[1]
    for p in range(gram.shape[0]):
        gram[p] = both[p * rows : (p + 1) * rows, :]
    acc[...] = jnp.zeros_like(acc)
    lane_at = lax.broadcasted_iota(jnp.int32, (rank, tile_rows), 1)
    for slot in range(slots):
        segment, code, limit = live_rows(list_ref, count_ref, visits_ref, slot, tile_rows)
        picked = split[:rank, pl.ds(pl.multiple_of(code * tile_cols, tile_cols), tile_cols)]
        contrib = bmm(picked, tiles[slot], 1, 1)
        acc[segment] += jnp.where(lane_at < limit, contrib, 0.0)
    whole = 1.0 / jnp.sum(profile, axis=0, keepdims=True)
    for segment in range(acc.shape[0]):
        value = acc[segment]
        column = jnp.sum(value, axis=0, keepdims=True) * whole
        col[segment : segment + 1, :] = column
        dev[segment] = (value - profile * column).astype(bf16)


def code_peer(me, distance, n_code):
    return lax.rem(me + distance, n_code)


def greet(n_pat, n_code, me_p, me_c):
    barrier = pltpu.get_barrier_semaphore()
    for d in range(1, n_code):
        pl.semaphore_signal(barrier, inc=1, device_id=(me_p, lax.rem(me_c + d, n_code)), device_id_type=MESH)
    for d in range(1, n_pat):
        pl.semaphore_signal(barrier, inc=1, device_id=(lax.rem(me_p + d, n_pat), me_c), device_id_type=MESH)
    pl.semaphore_wait(barrier, n_code + n_pat - 2)


def remote(src, dst, send, recv, where):
    copy = pltpu.make_async_remote_copy(
        src_ref=src, dst_ref=dst, send_sem=send, recv_sem=recv, device_id=where, device_id_type=MESH
    )
    copy.start()
    return copy


def exchange_kernel(
    n_pat, n_code, dev, col, gram, weight, dev_all, col_all, gram_all, weight_all, send_c, recv_c, send_p, recv_p, here
):
    me_p, me_c = lax.axis_index("pat"), lax.axis_index("code")
    own = dev.shape[0] // n_code
    greet(n_pat, n_code, me_p, me_c)
    copies = []
    for d in range(1, n_pat):
        copies.append(
            remote(weight, weight_all.at[me_p], send_p.at[0, d], recv_p.at[0, d], (lax.rem(me_p + d, n_pat), me_c))
        )
    rows = []
    for d in range(n_code - 1, 0, -1):
        to = lax.rem(me_c + d, n_code)
        where = (me_p, to)
        rows.append(
            remote(gram.at[me_p], gram_all.at[me_p, me_c], send_c.at[0, d], recv_c.at[0, d], where)
        )
    for d in range(n_code - 1, 0, -1):
        to = lax.rem(me_c + d, n_code)
        where = (me_p, to)
        copies.append(remote(col.at[pl.ds(to * own, own)], col_all.at[me_c], send_c.at[1, d], recv_c.at[1, d], where))
        copies.append(remote(dev.at[pl.ds(to * own, own)], dev_all.at[me_c], send_c.at[2, d], recv_c.at[2, d], where))
    local = [
        pltpu.make_async_copy(weight, weight_all.at[me_p], here.at[0]),
        pltpu.make_async_copy(gram.at[me_p], gram_all.at[me_p, me_c], here.at[1]),
        pltpu.make_async_copy(col.at[pl.ds(me_c * own, own)], col_all.at[me_c], here.at[2]),
        pltpu.make_async_copy(dev.at[pl.ds(me_c * own, own)], dev_all.at[me_c], here.at[3]),
    ]
    for copy in local:
        copy.start()
    for copy in local:
        copy.wait()
    for copy in rows:
        copy.wait_recv()
    slab = gram_all.at[me_p]
    for d in range(1, n_pat):
        copies.append(remote(slab, slab, send_p.at[1, d], recv_p.at[1, d], (lax.rem(me_p + d, n_pat), me_c)))
    for copy in copies:
        copy.wait()
    for copy in rows:
        copy.wait_send()


def polar_kernel(dev, col, gram, weight, mix, polar, projected, numer, inverse, code_gram):
    n_code, own, rank, tile_rows = dev.shape
    patients = own // VBLOCKS
    me_p, me_c = lax.axis_index("pat"), lax.axis_index("code")
    mine = [weight[me_p, pl.ds(me_c * patients + k, 1), :] for k in range(patients)]
    partials = [jnp.concatenate([gram[p, c] for p in range(gram.shape[0])], axis=0) for c in range(n_code)]
    sums = functools.reduce(jnp.add, partials)[:, :rank]
    code_gram[...] = sums
    weights = weight[...].reshape(-1, rank)
    inverse[...] = damped_inverse(sums * mm(weights, weights, 0, 0))
    products, iterates = [], []
    for k in range(patients):
        blocks = []
        for b in range(VBLOCKS):
            s = k * VBLOCKS + b
            value = None
            for c in range(n_code):
                term = dev[c, s].astype(f32) + partials[c][:, rank : rank + 1] * col[c, s : s + 1, :]
                value = term if value is None else value + term
            blocks.append(value)
        product = jnp.concatenate(blocks, axis=1)
        target = mm(mix[...] * mine[k], product)
        square = jnp.sum(jnp.sum(target * target, axis=1, keepdims=True), axis=0, keepdims=True)
        products.append(product)
        iterates.append(target / jnp.sqrt(square + epsilon))
    for step in range(NS_STEPS):
        grams = [mm(z, z, 1, 1) for z in iterates]
        iterates = [1.5 * z - 0.5 * mm(g, z) for g, z in zip(grams, iterates)]
    total = None
    for k in range(patients):
        polar[k] = iterates[k]
        value = mm(iterates[k], products[k], 1, 1)
        projected[k] = value
        term = value * mine[k]
        total = term if total is None else total + term
    numer[...] = total


def numer_kernel(n_pat, n_code, numer, result, pat_all, code_all, mid, send_p, recv_p, send_c, recv_c):
    me_p, me_c = lax.axis_index("pat"), lax.axis_index("code")
    greet(n_pat, n_code, me_p, me_c)
    copies = []
    for d in range(1, n_pat):
        copies.append(
            remote(numer, pat_all.at[me_p], send_p.at[d], recv_p.at[d], (lax.rem(me_p + d, n_pat), me_c))
        )
    pat_all[me_p] = numer[...]
    for copy in copies:
        copy.wait_recv()
    mid[...] = jnp.sum(pat_all[...], axis=0)
    more = []
    for d in range(1, n_code):
        more.append(
            remote(mid, code_all.at[me_c], send_c.at[d], recv_c.at[d], (me_p, lax.rem(me_c + d, n_code)))
        )
    code_all[me_c] = mid[...]
    for copy in more:
        copy.wait_recv()
    result[...] = jnp.sum(code_all[...], axis=0)
    for copy in copies + more:
        copy.wait_send()


def weight_kernel(numer, inverse, code_gram, polar, projected, mix_out, mix_gram, weight_out, spread):
    patients, rank, visits = polar.shape
    tile_rows = visits // VBLOCKS
    mix = mm(numer[...], inverse[...])
    mix_out[...] = mix
    square = mm(mix, mix, 0, 0)
    mix_gram[...] = square
    second = damped_inverse(square * code_gram[...])
    terms = jnp.concatenate(
        [jnp.sum(mix * projected[k], axis=0, keepdims=True) for k in range(patients)], axis=0
    )
    weight = jnp.maximum(mm(terms, second), 0.0)
    weight_out[...] = weight
    for k in range(patients):
        value = mm(mix * weight[k : k + 1, :], polar[k], 0, 0).astype(bf16)
        for b in range(VBLOCKS):
            spread[k * VBLOCKS + b] = value[:, b * tile_rows : (b + 1) * tile_rows]


def spread_kernel(
    n_pat, n_code, spread, weight, mix_gram, spread_all, inverse, weight_all, row, send_c, recv_c, send_p, recv_p, here
):
    me_p, me_c = lax.axis_index("pat"), lax.axis_index("code")
    greet(n_pat, n_code, me_p, me_c)
    first, bulk = [], []
    for d in range(1, n_code):
        where = (me_p, lax.rem(me_c + d, n_code))
        first.append(remote(weight, row.at[me_c], send_c.at[0, d], recv_c.at[0, d], where))
    for d in range(n_code - 1, 0, -1):
        where = (me_p, lax.rem(me_c + d, n_code))
        bulk.append(remote(spread, spread_all.at[me_c], send_c.at[1, d], recv_c.at[1, d], where))
    local = pltpu.make_async_copy(spread, spread_all.at[me_c], here.at[0])
    local.start()
    row[me_c] = weight[...]
    for copy in first:
        copy.wait_recv()
    second = []
    for d in range(1, n_pat):
        second.append(
            remote(row, weight_all.at[me_p], send_p.at[d], recv_p.at[d], (lax.rem(me_p + d, n_pat), me_c))
        )
    weight_all[me_p] = row[...]
    for copy in second:
        copy.wait_recv()
    rows = jnp.concatenate(
        [jnp.concatenate([weight_all[p, c] for c in range(n_code)], axis=0) for p in range(n_pat)], axis=0
    )
    inverse[...] = damped_inverse(mix_gram[...] * mm(rows, rows, 0, 0))
    for copy in bulk:
        copy.wait_recv()
    local.wait()
    for copy in first + second + bulk:
        copy.wait_send()


def code_kernel(list_ref, count_ref, visits_ref, tiles, spread, acc):
    slots, tile_rows, tile_cols = tiles.shape
    rank, codes = acc.shape
    acc[...] = jnp.zeros_like(acc)
    lane_at = lax.broadcasted_iota(jnp.int32, (rank, tile_rows), 1)
    for slot in range(slots):
        segment, code, limit = live_rows(list_ref, count_ref, visits_ref, slot, tile_rows)
        picked = jnp.where(lane_at < limit, spread[segment].astype(f32), 0.0).astype(bf16)
        where = pl.ds(pl.multiple_of(code * tile_cols, tile_cols), tile_cols)
        acc[:, where] += bmm(picked, tiles[slot])


def stacked_inverse(inverse):
    high = inverse.astype(bf16)
    low = (inverse - high.astype(f32)).astype(bf16)
    return jnp.concatenate([high, high, low], axis=1)


def solved_block(left, part):
    top = part.astype(bf16)
    rest = (part - top.astype(f32)).astype(bf16)
    return bmm(left, jnp.concatenate([top, rest, top], axis=0))


def solve_kernel(numer, inverse, result):
    codes = numer.shape[1]
    left = stacked_inverse(inverse[...])
    step = min(2048, codes)
    for start in range(0, codes, step):
        result[:, start : start + step] = solved_block(left, numer[:, start : start + step]).astype(bf16)


def quad_kernel(n_pat, numer, inverse, out, give, keep, pair, send_x, send_y, got_x, got_y, fin, sems, arrive):
    me_p, me_c = lax.axis_index("pat"), lax.axis_index("code")
    core, chip = lax.rem(me_p, 2), me_p // 2
    at_x, at_y = lax.rem(chip, 2), chip // 2
    width = numer.shape[1] // n_pat
    part = width // 2
    chips = [chip, at_y * 2 + 1 - at_x, (1 - at_y) * 2 + at_x, (1 - at_y) * 2 + 1 - at_x]
    partner = (chip * 2 + 1 - core, me_c)
    along_x, along_y = (chips[1] * 2 + core, me_c), (chips[2] * 2 + core, me_c)
    copies = []

    def lanes(index, half=None):
        if half is None:
            return pl.ds(pl.multiple_of(index * width, width), width)
        return pl.ds(pl.multiple_of(index * width + half * part, part), part)

    def go(src, dst, where):
        n = len(copies)
        copies.append(remote(src, dst, sems.at[n], arrive.at[n], where))
        return copies[-1]

    barrier = pltpu.get_barrier_semaphore()
    for where in (partner, along_x, along_y):
        pl.semaphore_signal(barrier, inc=1, device_id=where, device_id_type=MESH)
    pl.semaphore_wait(barrier, 3)

    left = stacked_inverse(inverse[...])
    order = (3, 1, 2, 0)
    pairs = {}
    for s in order:
        give[s] = solved_block(left, numer[:, lanes(chips[s] * 2 + 1 - core)]).astype(bf16)
        pairs[s] = go(give.at[s], pair.at[s], partner)
    for s in order:
        keep[s] = solved_block(left, numer[:, lanes(chips[s] * 2 + core)])
    for s in order:
        pairs[s].wait_recv()
        keep[s] += pair[s].astype(f32)
        if s == 3:
            send_x[0] = keep[3, :, :part].astype(bf16)
            x_far = go(send_x.at[0], got_x.at[0], along_x)
            send_y[0] = keep[3, :, part:].astype(bf16)
            y_far = go(send_y.at[0], got_y.at[0], along_y)
        elif s == 1:
            send_x[1] = keep[1, :, :part].astype(bf16)
            x_near = go(send_x.at[1], got_x.at[1], along_x)
        elif s == 2:
            send_y[1] = keep[2, :, part:].astype(bf16)
            y_near = go(send_y.at[1], got_y.at[1], along_y)
    x_far.wait_recv()
    send_y[2] = (keep[2, :, :part] + got_x[0].astype(f32)).astype(bf16)
    y_last = go(send_y.at[2], got_y.at[2], along_y)
    y_far.wait_recv()
    send_x[2] = (keep[1, :, part:] + got_y[0].astype(f32)).astype(bf16)
    x_last = go(send_x.at[2], got_x.at[2], along_x)
    x_near.wait_recv()
    y_last.wait_recv()
    low = keep[0, :, :part] + got_x[1].astype(f32) + got_y[2].astype(f32)
    fin[0] = jnp.maximum(low, 0.0).astype(bf16)
    spots = [out.at[:, lanes(me_p, h)] for h in range(2)]
    x_low = go(fin.at[0], spots[0], along_x)
    y_near.wait_recv()
    x_last.wait_recv()
    high = keep[0, :, part:] + got_y[1].astype(f32) + got_x[2].astype(f32)
    fin[1] = jnp.maximum(high, 0.0).astype(bf16)
    y_high = go(fin.at[1], spots[1], along_y)
    x_high = go(fin.at[1], spots[1], along_x)
    y_low = go(fin.at[0], spots[0], along_y)
    tail = [go(fin.at[0], spots[0], partner), go(fin.at[1], spots[1], partner)]
    out[:, lanes(me_p, 0)] = fin[0]
    out[:, lanes(me_p, 1)] = fin[1]

    def pass_on(s, half, where):
        spot = out.at[:, lanes(chips[s] * 2 + core, half)]
        return go(spot, spot, where)

    x_low.wait_recv()
    low_far = pass_on(1, 0, along_y)
    tail.append(pass_on(1, 0, partner))
    y_high.wait_recv()
    high_far = pass_on(2, 1, along_x)
    tail.append(pass_on(2, 1, partner))
    x_high.wait_recv()
    tail.append(pass_on(1, 1, partner))
    y_low.wait_recv()
    tail.append(pass_on(2, 0, partner))
    low_far.wait_recv()
    tail.append(pass_on(3, 0, partner))
    high_far.wait_recv()
    tail.append(pass_on(3, 1, partner))
    for copy in tail:
        copy.wait_recv()
    for copy in copies:
        copy.wait_send()


def reduce_kernel(n_pat, y, out, pair, half, got, send_a, recv_a, send_b, recv_b, send_c, recv_c, send_d, recv_d):
    me_p, me_c = lax.axis_index("pat"), lax.axis_index("code")
    chips = n_pat // 2
    chip, core = me_p // 2, lax.rem(me_p, 2)
    width = y.shape[1] // n_pat
    partner = (chip * 2 + 1 - core, me_c)

    def lanes(index):
        return pl.ds(pl.multiple_of(index * width, width), width)

    barrier = pltpu.get_barrier_semaphore()
    pl.semaphore_signal(barrier, inc=1, device_id=partner, device_id_type=MESH)
    for d in range(1, chips):
        pl.semaphore_signal(
            barrier, inc=1, device_id=(lax.rem(chip + d, chips) * 2 + core, me_c), device_id_type=MESH
        )
    pl.semaphore_wait(barrier, chips)

    order = list(range(1, chips)) + [0]
    stage_a, stage_b, stage_c, stage_d = [], [], [], []
    for d in order:
        q = lax.rem(chip + d, chips)
        stage_a.append(
            remote(y.at[:, lanes(q * 2 + 1 - core)], pair.at[d], send_a.at[d], recv_a.at[d], partner)
        )
    mine = None
    for n, d in enumerate(order):
        q = lax.rem(chip + d, chips)
        stage_a[n].wait_recv()
        value = y[:, lanes(q * 2 + core)].astype(f32) + pair[d].astype(f32)
        if d:
            half[d] = value.astype(bf16)
            stage_b.append(remote(half.at[d], got.at[d], send_b.at[d], recv_b.at[d], (q * 2 + core, me_c)))
        else:
            mine = value
    for copy in stage_b:
        copy.wait_recv()
    for d in range(1, chips):
        mine = mine + got[d].astype(f32)
    half[0] = jnp.maximum(mine, 0.0).astype(bf16)
    here = lanes(me_p)
    for d in range(1, chips):
        stage_c.append(
            remote(half.at[0], out.at[:, here], send_c.at[d], recv_c.at[d], (lax.rem(chip + d, chips) * 2 + core, me_c))
        )
    stage_d.append(remote(half.at[0], out.at[:, here], send_d.at[0], recv_d.at[0], partner))
    out[:, here] = half[0]
    for d in range(1, chips):
        stage_c[d - 1].wait_recv()
        q = lax.rem(chip + chips - d, chips)
        spot = out.at[:, lanes(q * 2 + core)]
        stage_d.append(remote(spot, spot, send_d.at[d], recv_d.at[d], partner))
    for copy in stage_d:
        copy.wait_recv()
    for copy in stage_a + stage_b + stage_c + stage_d:
        copy.wait_send()


def dma(*shape):
    return pltpu.SemaphoreType.DMA(shape)


def call(kernel, outs, n_in, scratch=(), smem=0, remote_id=None):
    if remote_id is None:
        params = pltpu.CompilerParams(vmem_limit_bytes=LIMIT)
    else:
        params = pltpu.CompilerParams(vmem_limit_bytes=LIMIT, collective_id=remote_id, has_side_effects=True)
    return pl.pallas_call(
        kernel,
        out_shape=[jax.ShapeDtypeStruct(s, d) for s, d in outs],
        in_specs=[SMEM] * smem + [VMEM] * (n_in - smem),
        out_specs=[VMEM] * len(outs),
        scratch_shapes=list(scratch),
        compiler_params=params,
    )


def body(tile_data, tile_list, tile_count, visit_counts, code_factor_t, visit_mix, patient_weight):
    n_pat, n_code = lax.axis_size("pat"), lax.axis_size("code")
    tiles = tile_data[0, 0]
    listing = tile_list[0, 0]
    count = tile_count[0]
    rank, codes = code_factor_t.shape
    slots, tile_rows, tile_cols = tiles.shape
    pat_row = visit_counts.shape[0]
    pat_own = pat_row // n_code
    segments, own = pat_row * VBLOCKS, pat_own * VBLOCKS
    chips = n_pat // 2
    width = codes // n_pat

    dev, col, gram = call(
        products_kernel,
        [((segments, rank, tile_rows), bf16), ((segments, tile_rows), f32), ((n_pat, rank // n_pat, 2 * rank), f32)],
        5,
        [pltpu.VMEM((2 * rank, codes), bf16), pltpu.VMEM((segments, rank, tile_rows), f32)],
        smem=3,
    )(listing, count, visit_counts, tiles, code_factor_t)
    dev_all, col_all, gram_all, weight_all = call(
        functools.partial(exchange_kernel, n_pat, n_code),
        [
            ((n_code, own, rank, tile_rows), bf16),
            ((n_code, own, tile_rows), f32),
            ((n_pat, n_code, rank // n_pat, 2 * rank), f32),
            ((n_pat, pat_row, rank), f32),
        ],
        4,
        [dma(3, n_code), dma(3, n_code), dma(2, n_pat), dma(2, n_pat), dma(4)],
        remote_id=1,
    )(dev, col, gram, patient_weight)
    square = ((rank, rank), f32)
    polar, projected, numer, inverse, code_gram = call(
        polar_kernel,
        [((pat_own, rank, VBLOCKS * tile_rows), f32), ((pat_own, rank, rank), f32), square, square, square],
        5,
    )(dev_all, col_all, gram_all, weight_all, visit_mix)
    (numer_sum,) = call(
        functools.partial(numer_kernel, n_pat, n_code),
        [square],
        1,
        [
            pltpu.VMEM((n_pat, rank, rank), f32),
            pltpu.VMEM((n_code, rank, rank), f32),
            pltpu.VMEM((rank, rank), f32),
            dma(n_pat),
            dma(n_pat),
            dma(n_code),
            dma(n_code),
        ],
        remote_id=2,
    )(numer)
    mix_new, mix_gram, weight_new, spread = call(
        weight_kernel, [square, square, ((pat_own, rank), f32), ((own, rank, tile_rows), bf16)], 5
    )(numer_sum, inverse, code_gram, polar, projected)
    spread_all, second = call(
        functools.partial(spread_kernel, n_pat, n_code),
        [((n_code, own, rank, tile_rows), bf16), square],
        3,
        [
            pltpu.VMEM((n_pat, n_code, pat_own, rank), f32),
            pltpu.VMEM((n_code, pat_own, rank), f32),
            dma(2, n_code),
            dma(2, n_code),
            dma(n_pat),
            dma(n_pat),
            dma(1),
        ],
        remote_id=3,
    )(spread, weight_new, mix_gram)
    (code_numer,) = call(code_kernel, [((rank, codes), f32)], 5, smem=3)(
        listing, count, visit_counts, tiles, spread_all.reshape(segments, rank, tile_rows)
    )
    if chips == 4:
        (code_new,) = call(
            functools.partial(quad_kernel, n_pat),
            [((rank, codes), bf16)],
            2,
            [
                pltpu.VMEM((chips, rank, width), bf16),
                pltpu.VMEM((chips, rank, width), f32),
                pltpu.VMEM((chips, rank, width), bf16),
                pltpu.VMEM((3, rank, width // 2), bf16),
                pltpu.VMEM((3, rank, width // 2), bf16),
                pltpu.VMEM((3, rank, width // 2), bf16),
                pltpu.VMEM((3, rank, width // 2), bf16),
                pltpu.VMEM((2, rank, width // 2), bf16),
                dma(24),
                dma(24),
            ],
            remote_id=4,
        )(code_numer, second)
    else:
        (solved,) = call(solve_kernel, [((rank, codes), bf16)], 2)(code_numer, second)
        (code_new,) = call(
            functools.partial(reduce_kernel, n_pat),
            [((rank, codes), bf16)],
            1,
            [pltpu.VMEM((chips, rank, width), bf16)] * 3 + [dma(chips)] * 8,
            remote_id=4,
        )(solved)
    return (code_new.astype(f32), mix_new, weight_new)


def solution(mesh):
    placed = (
        P("pat", "code", None, None, None),
        P("pat", "code", None, None),
        P("pat", "code"),
        P("pat"),
        P(None, "code"),
        P(),
        P("pat", None),
    )
    return jax.shard_map(
        body,
        mesh=mesh,
        in_specs=placed,
        out_specs=(P(None, "code"), P(), P(("pat", "code"), None)),
        check_vma=False,
    )
```

profile of v0, /device:TPU:0, one launch (start us, length us, event | category | flops | bytes accessed | tf_op | source)
XLA Modules:
  0.0 117.7 jit_solution(1515732350788582847)
XLA Ops:
  1.3 1.3 %copy.12 = s32[1,1,3,16]{3,2,1,0:T(4,128)} copy(s32[1,1,3,16]{3,1,2,0:T(1,128)} %param.8) | data formatting | bytes 384
  2.5 6.3 %shard_map.94 = (bf16[32,64,128]{2,1,0:T(8,128)(2,1)}, f32[32,128]{1,0:T(8,128)}, f32[8,8,128]{2,1,0:T(8,128)}) custom-call(s32[3,16]{1,0:T(4,128)} %bitcast.11, s32[1]{0:T(128)} %bitcast.6.count_ref, s32[16]{0:T(128)} %visits_ref.3, bf16[16,128,512]{2,1,0:T(8,128)(2,1)} %bitcast.8, f32[64,16384]{1,0:T(8,128)} %factor.1), custom_call_target="tpu_custom_call" | custom-call | tf_op jit(solution)/shard_map/pallas_call | solution.py:504
  8.9 21.9 %shard_map.95 = (bf16[4,8,64,128]{3,2,1,0:T(8,128)(2,1)}, f32[4,8,128]{2,1,0:T(8,128)}, f32[8,4,8,128]{3,2,1,0:T(8,128)}, f32[8,16,64]{2,1,0:T(8,128)}) custom-call(bf16[32,64,128]{2,1,0:T(8,128)(2,1)} %get-tuple-element.21.dev, f32[32,128]{1,0:T(8,128)} %get-tuple-element.22.col, f32[8,8,128]{2,1,0:T(8,128)} %get-tuple-element.23.gram, f32[16,64]{1,0:T(8,128)} %weight.1), custom_call_target="tpu_custom_call" | custom-call | tf_op jit(solution)/shard_map/pallas_call | solution.py:511
  30.8 9.6 %shard_map.96 = (f32[4,64,256]{2,1,0:T(8,128)}, f32[4,64,64]{2,1,0:T(8,128)}, f32[64,64]{1,0:T(8,128)}, f32[64,64]{1,0:T(8,128)}, f32[64,64]{1,0:T(8,128)}) custom-call(bf16[4,8,64,128]{3,2,1,0:T(8,128)(2,1)} %get-tuple-element.24.dev, f32[4,8,128]{2,1,0:T(8,128)} %get-tuple-element.25.col, f32[8,4,8,128]{3,2,1,0:T(8,128)} %get-tuple-element.26.gram, ...), custom_call_target="tpu_custom_call" | custom-call | tf_op jit(solution)/shard_map/pallas_call | solution.py:524
  40.5 11.6 %shard_map.97.numer = f32[64,64]{1,0:T(8,128)} custom-call(f32[64,64]{1,0:T(8,128)} %get-tuple-element.28.numer), custom_call_target="tpu_custom_call" | custom-call | tf_op jit(solution)/shard_map/pallas_call | solution.py:529
  52.0 10.2 %shard_map.98 = (f32[64,64]{1,0:T(8,128)}, f32[64,64]{1,0:T(8,128)}, f32[4,64]{1,0:T(4,128)}, bf16[8,64,128]{2,1,0:T(8,128)(2,1)}) custom-call(f32[64,64]{1,0:T(8,128)} %shard_map.97.numer, f32[64,64]{1,0:T(8,128)} %get-tuple-element.29.inverse, f32[64,64]{1,0:T(8,128)} %get-tuple-element.30.code_gram, f32[4,64,256]{2,1,0:T(8,128)} %get-tuple-element.31.polar, ...), custom_call_target="tpu_custom_call" | custom-call | tf_op jit(solution)/shard_map/pallas_call | solution.py:544
  62.2 19.2 %shard_map.99 = (bf16[4,8,64,128]{3,2,1,0:T(8,128)(2,1)}, f32[64,64]{1,0:T(8,128)}) custom-call(bf16[8,64,128]{2,1,0:T(8,128)(2,1)} %get-tuple-element.33.spread, f32[4,64]{1,0:T(4,128)} %get-tuple-element.20.weight, f32[64,64]{1,0:T(8,128)} %get-tuple-element.35.mix_gram), custom_call_target="tpu_custom_call" | custom-call | tf_op jit(solution)/shard_map/pallas_call | solution.py:547
  81.4 4.4 %shard_map.100.numer = f32[64,16384]{1,0:T(8,128)} custom-call(s32[3,16]{1,0:T(4,128)} %bitcast.12, s32[1]{0:T(128)} %bitcast.7.count_ref, s32[16]{0:T(128)} %visits_ref.3, bf16[16,128,512]{2,1,0:T(8,128)(2,1)} %bitcast.9, bf16[32,64,128]{2,1,0:T(8,128)(2,1)} %bitcast.10), custom_call_target="tpu_custom_call" | custom-call | tf_op jit(solution)/shard_map/pallas_call | solution.py:562
  85.8 28.0 %shard_map.101 = bf16[64,16384]{1,0:T(8,128)(2,1)} custom-call(f32[64,16384]{1,0:T(8,128)} %shard_map.100.numer, f32[64,64]{1,0:T(8,128)} %get-tuple-element.37.inverse), custom_call_target="tpu_custom_call" | custom-call | tf_op jit(solution)/shard_map/pallas_call | solution.py:566
  113.8 3.9 %convert_element_type.3 = f32[64,16384]{1,0:T(8,128)} convert(bf16[64,16384]{1,0:T(8,128)(2,1)} %shard_map.101) | non-fusion elementwise | flops 1048576 | bytes 6291456 | tf_op jit(solution)/shard_map/convert_element_type | solution.py:593
where the time goes:
time: 119 us; the launch traced here: 118 us
  Pallas kernels  111 us (93%)
  other arithmetic  3.88 us (3%)
  between operations  1.31 us (1%)
  local copies, waits for them, and re-layouts  1.26 us (1%)
    pallas_call x1, Pallas kernels, body(): call(functools.partial(quad_kernel, n_pat), [((rank, codes), bf16)], 2, [...  28 us
    pallas_call x1, Pallas kernels, body(): call(functools.partial(exchange_kernel, n_pat, n_code), [((n_code, own, r...  21.9 us
    pallas_call x1, Pallas kernels, body(): call(functools.partial(spread_kernel, n_pat, n_code), [((n_code, own, ran...  19.2 us
    pallas_call x1, Pallas kernels, body(): call(functools.partial(numer_kernel, n_pat, n_code), [square], 1, [pltpu....  11.6 us
    pallas_call x1, Pallas kernels, body(): call(weight_kernel, [square, square, ((pat_own, rank), f32), ((own, rank,...  10.2 us
    pallas_call x1, Pallas kernels, body(): call(polar_kernel, [((pat_own, rank, VBLOCKS * tile_rows), f32), ((pat_ow...  9.64 us
    pallas_call x1, Pallas kernels, body(): call(products_kernel, [((segments, rank, tile_rows), bf16), ((segments, t...  6.34 us
    pallas_call x1, Pallas kernels, body(): call(code_kernel, [((rank, codes), f32)], 5, smem=3)  4.39 us

commit v1 on v0

--- a/solution.py
+++ b/solution.py
@@ -9,6 +9,7 @@
 
 VBLOCKS = 2
 NS_STEPS = 8
+INVERSE_STEPS = 8
 MESH = pl.DeviceIdType.MESH
 damping = 0.1
 epsilon = 1e-06
@@ -17,7 +18,7 @@
 bf16 = jnp.bfloat16
 VMEM = pl.BlockSpec(memory_space=pltpu.VMEM)
 SMEM = pl.BlockSpec(memory_space=pltpu.SMEM)
-LIMIT = 60 * 1024 * 1024
+LIMIT = 32 * 1024 * 1024
 
 
 def mm(left, right, left_dim=1, right_dim=0):
@@ -40,28 +41,31 @@
     size = gram.shape[0]
     row_at = lax.broadcasted_iota(jnp.int32, (size, size), 0)
     lane_at = lax.broadcasted_iota(jnp.int32, (size, size), 1)
-    lane_one = lax.broadcasted_iota(jnp.int32, (1, size), 1)
-    on_diag = row_at == lane_at
-    trace = jnp.sum(jnp.sum(jnp.where(on_diag, gram, 0.0), axis=1, keepdims=True), axis=0, keepdims=True)
-    a = gram + jnp.where(on_diag, trace * (damping / size), 0.0)
-    for k in range(0, size, 2):
-        row_p, row_q = a[k : k + 1, :], a[k + 1 : k + 2, :]
-        col_p, col_q = a[:, k : k + 1], a[:, k + 1 : k + 2]
-        pp, pq, qq = a[k : k + 1, k : k + 1], a[k : k + 1, k + 1 : k + 2], a[k + 1 : k + 2, k + 1 : k + 2]
-        scale = 1.0 / (pp * qq - pq * pq)
-        at_p, at_q = lane_one == k, lane_one == k + 1
-        row_p = jnp.where(at_p, 1.0, jnp.where(at_q, 0.0, row_p))
-        row_q = jnp.where(at_q, 1.0, jnp.where(at_p, 0.0, row_q))
-        new_p = (qq * scale) * row_p - (pq * scale) * row_q
-        new_q = (pp * scale) * row_q - (pq * scale) * row_p
-        kept = jnp.where((lane_at == k) | (lane_at == k + 1), 0.0, a)
-        a = kept - col_p * new_p - col_q * new_q
-        a = jnp.where(row_at == k, new_p, jnp.where(row_at == k + 1, new_q, a))
-    return a
+    eye = jnp.where(row_at == lane_at, 1.0, 0.0)
+    trace = jnp.sum(jnp.sum(gram * eye, axis=1, keepdims=True), axis=0, keepdims=True)
+    mean = trace * (1.0 / size)
+    unscale = 1.0 / (mean * (0.5 * size + damping))
+    a = gram * unscale + eye * (damping / (0.5 * size + damping))
+    rest = eye - a
+    tau = (size + 2.0 * damping) / size
+    x = eye
+    for step in range(INVERSE_STEPS):
+        twice = 2.0 * tau * tau
+        gain = twice / (twice - 1.0)
+        if step == 0:
+            x, square = x + rest, mm(rest, rest)
+        else:
+            both = mm(rest, jnp.concatenate([x, rest], axis=1))
+            x, square = x + both[:, :size], both[:, size:]
+        x = x * gain
+        rest = square * gain - eye * (1.0 / (twice - 1.0))
+        tau = twice - 1.0
+    x = x + mm(x, eye - mm(a, x))
+    return x * unscale
 
 
 def live_rows(list_ref, count_ref, visits_ref, slot, tile_rows):
-    owner, block, code = list_ref[0, slot], list_ref[1, slot], list_ref[2, slot]
+    owner, block, code = list_ref[0, 0, slot], list_ref[1, 0, slot], list_ref[2, 0, slot]
     limit = jnp.where(slot < count_ref[0], visits_ref[owner] - block * tile_rows, 0)
     return owner * VBLOCKS + block, code, limit
 
@@ -491,7 +495,7 @@
 def body(tile_data, tile_list, tile_count, visit_counts, code_factor_t, visit_mix, patient_weight):
     n_pat, n_code = lax.axis_size("pat"), lax.axis_size("code")
     tiles = tile_data[0, 0]
-    listing = tile_list[0, 0]
+    listing = jnp.transpose(tile_list[0], (1, 0, 2))
     count = tile_count[0]
     rank, codes = code_factor_t.shape
     slots, tile_rows, tile_cols = tiles.shape

time: 119 us -> 95.4 us (0.80)
  Pallas kernels: 111 us -> 85.6 us
  local copies, waits for them, and re-layouts: 1.26 us -> 5.81 us
  other arithmetic: 3.88 us -> 2.29 us
    pallas_call x1, Pallas kernels: 10.2 us -> 3.41 us  [body(): call(weight_kernel, [square, square, ((pat_own, rank), f32), ((own, rank,...]
    unnamed x1 -> x20, local copies, waits for them, and re-layouts: 1.26 us -> 5.81 us
    pallas_call x1, Pallas kernels: 19.2 us -> 15.8 us  [body(): call(functools.partial(spread_kernel, n_pat, n_code), [((n_code, own, ran...]
    pallas_call x1, Pallas kernels: 28 us -> 24.8 us  [body(): call(functools.partial(quad_kernel, n_pat), [((rank, codes), bf16)], 2, [...]
    pallas_call x1, Pallas kernels: 4.39 us -> 1.28 us  [body(): call(code_kernel, [((rank, codes), f32)], 5, smem=3)]
    pallas_call x1, Pallas kernels: 9.64 us -> 6.65 us  [body(): call(polar_kernel, [((pat_own, rank, VBLOCKS * tile_rows), f32), ((pat_ow...]
    pallas_call x1, Pallas kernels: 6.34 us -> 3.36 us  [body(): call(products_kernel, [((segments, rank, tile_rows), bf16), ((segments, t...]
    pallas_call x1, Pallas kernels: 21.9 us -> 20.1 us  [body(): call(functools.partial(exchange_kernel, n_pat, n_code), [((n_code, own, r...]
where the time goes in v1:
time: 95.4 us; the launch traced here: 95.1 us
  Pallas kernels  85.6 us (90%)
  local copies, waits for them, and re-layouts  5.81 us (6%)
  other arithmetic  2.29 us (2%)
  between operations  1.4 us (1%)
    pallas_call x1, Pallas kernels, body(): call(functools.partial(quad_kernel, n_pat), [((rank, codes), bf16)], 2, [...  24.8 us
    pallas_call x1, Pallas kernels, body(): call(functools.partial(exchange_kernel, n_pat, n_code), [((n_code, own, r...  20.1 us
    pallas_call x1, Pallas kernels, body(): call(functools.partial(spread_kernel, n_pat, n_code), [((n_code, own, ran...  15.8 us
    pallas_call x1, Pallas kernels, body(): call(functools.partial(numer_kernel, n_pat, n_code), [square], 1, [pltpu....  10.3 us
    pallas_call x1, Pallas kernels, body(): call(polar_kernel, [((pat_own, rank, VBLOCKS * tile_rows), f32), ((pat_ow...  6.65 us
    unnamed x20, local copies, waits for them, and re-layouts  5.81 us
    pallas_call x1, Pallas kernels, body(): call(weight_kernel, [square, square, ((pat_own, rank), f32), ((own, rank,...  3.41 us
    pallas_call x1, Pallas kernels, body(): call(products_kernel, [((segments, rank, tile_rows), bf16), ((segments, t...  3.36 us

profile of v1, /device:TPU:0, one launch (start us, length us, event | category | flops | bytes accessed | tf_op | source)
XLA Modules:
  0.0 95.1 jit_solution(13927018332074250536)
XLA Ops:
  0.6 0.0 copy-start.4
  1.3 0.0 copy-start
  1.3 1.6 %copy-done = bf16[1,1,16,128,512]{4,3,2,1,0:T(8,128)(2,1)S(1)} copy-done((bf16[1,1,16,128,512]{4,3,2,1,0:T(8,128)(2,1)S(1)}, bf16[1,1,16,128,512]{4,3,2,1,0:T(8,128)(2,1)}, u32[]{:S(2)}) %copy-start) | copy-done | bytes 2097176
  2.9 0.0 copy-start.2
  2.9 2.2 %copy-done.2 = f32[64,16384]{1,0:T(8,128)S(1)} copy-done((f32[64,16384]{1,0:T(8,128)S(1)}, f32[64,16384]{1,0:T(8,128)}, u32[]{:S(2)}) %copy-start.2) | copy-done | bytes 4194328
  5.1 0.0 copy-start.5
  5.1 0.7 copy-done.5
  5.8 0.0 copy-start.7
  5.8 0.7 copy-done.7
  6.4 0.0 copy-start.3
  6.4 0.0 copy-start.1
  6.4 0.0 copy-start.6
  6.4 0.0 copy-start.8
  6.4 3.4 %shard_map.94 = (bf16[32,64,128]{2,1,0:T(8,128)(2,1)S(1)}, f32[32,128]{1,0:T(8,128)S(1)}, f32[8,8,128]{2,1,0:T(8,128)S(1)}) custom-call(s32[3,1,16]{2,1,0:T(1,128)S(1)} %bitcast.9, s32[1]{0:T(128)} %bitcast.4.count_ref, s32[16]{0:T(128)S(1)} %copy-done.7, bf16[16,128,512]{2,1,0:T(8,128)(2,1)S(1)} %bitcast.6, f32[64,16384]{1,0:T(8,128)S(1)} %copy-done.2), custom_call_target="tpu_custom_call" | custom-call | tf_op jit(solution)/shard_map/pallas_call | solution.py:508
  9.8 0.0 copy-done.4
  9.8 20.1 %shard_map.95 = (bf16[4,8,64,128]{3,2,1,0:T(8,128)(2,1)S(1)}, f32[4,8,128]{2,1,0:T(8,128)S(1)}, f32[8,4,8,128]{3,2,1,0:T(8,128)S(1)}, f32[8,16,64]{2,1,0:T(8,128)S(1)}) custom-call(bf16[32,64,128]{2,1,0:T(8,128)(2,1)S(1)} %get-tuple-element.21.dev, f32[32,128]{1,0:T(8,128)S(1)} %get-tuple-element.22.col, f32[8,8,128]{2,1,0:T(8,128)S(1)} %get-tuple-element.23.gram, ...), custom_call_target="tpu_custom_call" | custom-call | tf_op jit(solution)/shard_map/pallas_call | solution.py:515
  29.9 0.0 copy-done.3
  29.9 6.6 %shard_map.96 = (f32[4,64,256]{2,1,0:T(8,128)S(1)}, f32[4,64,64]{2,1,0:T(8,128)S(1)}, f32[64,64]{1,0:T(8,128)S(1)}, f32[64,64]{1,0:T(8,128)S(1)}, f32[64,64]{1,0:T(8,128)S(1)}) custom-call(bf16[4,8,64,128]{3,2,1,0:T(8,128)(2,1)S(1)} %get-tuple-element.24.dev, f32[4,8,128]{2,1,0:T(8,128)S(1)} %get-tuple-element.25.col, ...), custom_call_target="tpu_custom_call" | custom-call | tf_op jit(solution)/shard_map/pallas_call | solution.py:528
  36.6 10.3 %shard_map.97.numer = f32[64,64]{1,0:T(8,128)S(1)} custom-call(f32[64,64]{1,0:T(8,128)S(1)} %get-tuple-element.28.numer), custom_call_target="tpu_custom_call" | custom-call | tf_op jit(solution)/shard_map/pallas_call | solution.py:533
  46.8 3.4 %shard_map.98 = (f32[64,64]{1,0:T(8,128)}, f32[64,64]{1,0:T(8,128)S(1)}, f32[4,64]{1,0:T(4,128)}, bf16[8,64,128]{2,1,0:T(8,128)(2,1)S(1)}) custom-call(f32[64,64]{1,0:T(8,128)S(1)} %shard_map.97.numer, f32[64,64]{1,0:T(8,128)S(1)} %get-tuple-element.29.inverse, f32[64,64]{1,0:T(8,128)S(1)} %get-tuple-element.30.code_gram, ...), custom_call_target="tpu_custom_call" | custom-call | tf_op jit(solution)/shard_map/pallas_call | solution.py:548
  50.3 0.0 copy-start.9
  50.3 0.7 copy-done.9
  50.9 15.8 %shard_map.99 = (bf16[4,8,64,128]{3,2,1,0:T(8,128)(2,1)S(1)}, f32[64,64]{1,0:T(8,128)S(1)}) custom-call(bf16[8,64,128]{2,1,0:T(8,128)(2,1)S(1)} %get-tuple-element.33.spread, f32[4,64]{1,0:T(4,128)S(1)} %copy-done.9, f32[64,64]{1,0:T(8,128)S(1)} %get-tuple-element.35.mix_gram), custom_call_target="tpu_custom_call" | custom-call | tf_op jit(solution)/shard_map/pallas_call | solution.py:551
  66.7 0.0 copy-done.1
  66.7 0.0 copy-done.6
  66.7 0.0 copy-done.8
  66.8 1.3 %shard_map.100.numer = f32[64,16384]{1,0:T(8,128)S(1)} custom-call(s32[3,1,16]{2,1,0:T(1,128)S(1)} %bitcast.10, s32[1]{0:T(128)} %bitcast.5.count_ref, s32[16]{0:T(128)S(1)} %copy-done.8, bf16[16,128,512]{2,1,0:T(8,128)(2,1)S(1)} %bitcast.7, bf16[32,64,128]{2,1,0:T(8,128)(2,1)S(1)} %bitcast.8), custom_call_target="tpu_custom_call" | custom-call | tf_op jit(solution)/shard_map/pallas_call | solution.py:566
  68.0 24.8 %shard_map.101 = bf16[64,16384]{1,0:T(8,128)(2,1)S(1)} custom-call(f32[64,16384]{1,0:T(8,128)S(1)} %shard_map.100.numer, f32[64,64]{1,0:T(8,128)S(1)} %get-tuple-element.37.inverse), custom_call_target="tpu_custom_call" | custom-call | tf_op jit(solution)/shard_map/pallas_call | solution.py:570
  92.8 2.3 %convert_element_type.3 = f32[64,16384]{1,0:T(8,128)} convert(bf16[64,16384]{1,0:T(8,128)(2,1)S(1)} %shard_map.101) | non-fusion elementwise | flops 1048576 | bytes 6291456 | tf_op jit(solution)/shard_map/convert_element_type | solution.py:597
Async XLA Ops:
  0.6 9.2 %copy-start.4 = (f32[16,64]{1,0:T(8,128)S(1)}, f32[16,64]{1,0:T(8,128)}, u32[]{:S(2)}) copy-start(f32[16,64]{1,0:T(8,128)} %weight.1) | copy-start | bytes 12292
  1.3 1.6 %copy-start = (bf16[1,1,16,128,512]{4,3,2,1,0:T(8,128)(2,1)S(1)}, bf16[1,1,16,128,512]{4,3,2,1,0:T(8,128)(2,1)}, u32[]{:S(2)}) copy-start(bf16[1,1,16,128,512]{4,3,2,1,0:T(8,128)(2,1)} %param.7) | copy-start | bytes 6291460
  2.9 2.2 %copy-start.2 = (f32[64,16384]{1,0:T(8,128)S(1)}, f32[64,16384]{1,0:T(8,128)}, u32[]{:S(2)}) copy-start(f32[64,16384]{1,0:T(8,128)} %factor.1) | copy-start | bytes 12582916
  5.1 0.7 copy-start.5
  5.8 0.7 copy-start.7
  6.4 23.5 %copy-start.3 = (f32[64,64]{1,0:T(8,128)S(1)}, f32[64,64]{1,0:T(8,128)}, u32[]{:S(2)}) copy-start(f32[64,64]{1,0:T(8,128)} %mix.1) | copy-start | bytes 49156
  6.4 60.3 %copy-start.1 = (bf16[1,1,16,128,512]{4,3,2,1,0:T(8,128)(2,1)S(1)}, bf16[1,1,16,128,512]{4,3,2,1,0:T(8,128)(2,1)}, u32[]{:S(2)}) copy-start(bf16[1,1,16,128,512]{4,3,2,1,0:T(8,128)(2,1)} %param.7) | copy-start | bytes 6291460
  6.4 60.3 %copy-start.6 = (s32[1,1,3,16]{3,1,2,0:T(1,128)S(1)}, s32[1,1,3,16]{3,1,2,0:T(1,128)}, u32[]{:S(2)}) copy-start(s32[1,1,3,16]{3,1,2,0:T(1,128)} %param.8) | copy-start | bytes 580
  6.4 60.3 %copy-start.8 = (s32[16]{0:T(128)S(1)}, s32[16]{0:T(128)}, u32[]{:S(2)}) copy-start(s32[16]{0:T(128)} %visits_ref.3) | copy-start | bytes 196
  50.3 0.7 copy-start.9

commit v2 on v1

--- a/solution.py
+++ b/solution.py
@@ -126,169 +126,175 @@
     return copy
 
 
-def exchange_kernel(
-    n_pat, n_code, dev, col, gram, weight, dev_all, col_all, gram_all, weight_all, send_c, recv_c, send_p, recv_p, here
+def polar_factors(products, mix, mine):
+    rank = mix.shape[0]
+    row_at = lax.broadcasted_iota(jnp.int32, (rank, rank), 0)
+    lane_at = lax.broadcasted_iota(jnp.int32, (rank, rank), 1)
+    eye = jnp.where(row_at == lane_at, 1.0, 0.0)
+    targets = [mm(mix * w, x) for w, x in zip(mine, products)]
+    crosses, grams, scales = [], [], []
+    for target, product in zip(targets, products):
+        both = mm(target, jnp.concatenate([target, product], axis=0), 1, 1)
+        gram = both[:, :rank]
+        norm = jnp.sum(jnp.sum(gram * eye, axis=1, keepdims=True), axis=0, keepdims=True) + epsilon
+        crosses.append(both[:, rank:])
+        grams.append(gram / norm)
+        scales.append(1.0 / jnp.sqrt(norm))
+    maps = None
+    for step in range(NS_STEPS):
+        steps = [1.5 * eye - 0.5 * g for g in grams]
+        if step == 0:
+            maps, halves = steps, [mm(p, g) for p, g in zip(steps, grams)]
+        elif step < NS_STEPS - 1:
+            wide = [mm(p, jnp.concatenate([g, q], axis=1)) for p, g, q in zip(steps, grams, maps)]
+            halves, maps = [w[:, :rank] for w in wide], [w[:, rank:] for w in wide]
+        else:
+            maps = [mm(p, q) for p, q in zip(steps, maps)]
+        if step < NS_STEPS - 1:
+            grams = [mm(h, p) for h, p in zip(halves, steps)]
+    maps = [q * scale for q, scale in zip(maps, scales)]
+    polars = [mm(q, target) for q, target in zip(maps, targets)]
+    return polars, [mm(q, cross) for q, cross in zip(maps, crosses)]
+
+
+def core_kernel(
+    n_pat,
+    n_code,
+    dev,
+    col,
+    gram,
+    weight,
+    mix_in,
+    spread,
+    inverse,
+    mix_out,
+    weight_out,
+    dev_all,
+    col_all,
+    gram_all,
+    old_all,
+    numer_c,
+    numer_p,
+    mid,
+    polar_all,
+    row,
+    weight_all,
+    send_c,
+    recv_c,
+    send_p,
+    recv_p,
 ):
     me_p, me_c = lax.axis_index("pat"), lax.axis_index("code")
-    own = dev.shape[0] // n_code
+    segments, rank, tile_rows = dev.shape
+    own = segments // n_code
+    patients = own // VBLOCKS
+    half = rank // 2
+
+    def to_code(kind, src, dst):
+        copies = []
+        for d in range(n_code - 1, 0, -1):
+            where = (me_p, lax.rem(me_c + d, n_code))
+            copies.append(remote(src(d), dst, send_c.at[kind, d], recv_c.at[kind, d], where))
+        return copies
+
+    def to_pat(kind, src, dst):
+        copies = []
+        for d in range(1, n_pat):
+            where = (lax.rem(me_p + d, n_pat), me_c)
+            copies.append(remote(src, dst, send_p.at[kind, d], recv_p.at[kind, d], where))
+        return copies
+
+    def share(d):
+        return pl.ds(lax.rem(me_c + d, n_code) * own, own)
+
     greet(n_pat, n_code, me_p, me_c)
-    copies = []
-    for d in range(1, n_pat):
-        copies.append(
-            remote(weight, weight_all.at[me_p], send_p.at[0, d], recv_p.at[0, d], (lax.rem(me_p + d, n_pat), me_c))
-        )
-    rows = []
-    for d in range(n_code - 1, 0, -1):
-        to = lax.rem(me_c + d, n_code)
-        where = (me_p, to)
-        rows.append(
-            remote(gram.at[me_p], gram_all.at[me_p, me_c], send_c.at[0, d], recv_c.at[0, d], where)
-        )
-    for d in range(n_code - 1, 0, -1):
-        to = lax.rem(me_c + d, n_code)
-        where = (me_p, to)
-        copies.append(remote(col.at[pl.ds(to * own, own)], col_all.at[me_c], send_c.at[1, d], recv_c.at[1, d], where))
-        copies.append(remote(dev.at[pl.ds(to * own, own)], dev_all.at[me_c], send_c.at[2, d], recv_c.at[2, d], where))
-    local = [
-        pltpu.make_async_copy(weight, weight_all.at[me_p], here.at[0]),
-        pltpu.make_async_copy(gram.at[me_p], gram_all.at[me_p, me_c], here.at[1]),
-        pltpu.make_async_copy(col.at[pl.ds(me_c * own, own)], col_all.at[me_c], here.at[2]),
-        pltpu.make_async_copy(dev.at[pl.ds(me_c * own, own)], dev_all.at[me_c], here.at[3]),
-    ]
-    for copy in local:
-        copy.start()
-    for copy in local:
-        copy.wait()
-    for copy in rows:
-        copy.wait_recv()
-    slab = gram_all.at[me_p]
-    for d in range(1, n_pat):
-        copies.append(remote(slab, slab, send_p.at[1, d], recv_p.at[1, d], (lax.rem(me_p + d, n_pat), me_c)))
-    for copy in copies:
-        copy.wait()
-    for copy in rows:
-        copy.wait_send()
-
-
-def polar_kernel(dev, col, gram, weight, mix, polar, projected, numer, inverse, code_gram):
-    n_code, own, rank, tile_rows = dev.shape
-    patients = own // VBLOCKS
-    me_p, me_c = lax.axis_index("pat"), lax.axis_index("code")
-    mine = [weight[me_p, pl.ds(me_c * patients + k, 1), :] for k in range(patients)]
-    partials = [jnp.concatenate([gram[p, c] for p in range(gram.shape[0])], axis=0) for c in range(n_code)]
-    sums = functools.reduce(jnp.add, partials)[:, :rank]
-    code_gram[...] = sums
-    weights = weight[...].reshape(-1, rank)
-    inverse[...] = damped_inverse(sums * mm(weights, weights, 0, 0))
-    products, iterates = [], []
+    gram_c = to_code(0, lambda d: gram.at[me_p], gram_all.at[me_p, me_c])
+    col_c = to_code(1, lambda d: col.at[share(d)], col_all.at[me_c])
+    dev_c = to_code(2, lambda d: dev.at[share(d)], dev_all.at[me_c])
+    old_p = to_pat(0, weight, old_all.at[me_p])
+    gram_all[me_p, me_c] = gram[me_p]
+    old_all[me_p] = weight[...]
+    col_all[me_c] = col[share(0)]
+    dev_all[me_c] = dev[share(0)]
+    for copy in gram_c:
+        copy.wait_recv()
+    gram_p = to_pat(1, gram_all.at[me_p], gram_all.at[me_p])
+    for copy in old_p + gram_p:
+        copy.wait_recv()
+    partials = [jnp.concatenate([gram_all[p, c] for p in range(n_pat)], axis=0) for c in range(n_code)]
+    code_gram = functools.reduce(jnp.add, partials)[:, :rank]
+    olds = old_all[...].reshape(-1, rank)
+    first = damped_inverse(code_gram * mm(olds, olds, 0, 0))
+    mine = [weight[pl.ds(me_c * patients + k, 1), :] for k in range(patients)]
+
+    for copy in col_c + dev_c:
+        copy.wait_recv()
+    products = []
     for k in range(patients):
         blocks = []
         for b in range(VBLOCKS):
             s = k * VBLOCKS + b
             value = None
             for c in range(n_code):
-                term = dev[c, s].astype(f32) + partials[c][:, rank : rank + 1] * col[c, s : s + 1, :]
+                term = dev_all[c, s].astype(f32) + partials[c][:, rank : rank + 1] * col_all[c, s : s + 1, :]
                 value = term if value is None else value + term
             blocks.append(value)
-        product = jnp.concatenate(blocks, axis=1)
-        target = mm(mix[...] * mine[k], product)
-        square = jnp.sum(jnp.sum(target * target, axis=1, keepdims=True), axis=0, keepdims=True)
-        products.append(product)
-        iterates.append(target / jnp.sqrt(square + epsilon))
-    for step in range(NS_STEPS):
-        grams = [mm(z, z, 1, 1) for z in iterates]
-        iterates = [1.5 * z - 0.5 * mm(g, z) for g, z in zip(grams, iterates)]
-    total = None
+        products.append(jnp.concatenate(blocks, axis=1))
+    polars, projected = polar_factors(products, mix_in[...], mine)
+    total = functools.reduce(jnp.add, [p * w for p, w in zip(projected, mine)])
+    numer_c[me_c] = jnp.concatenate([total[:half], total[half:]], axis=1)
+    numer_z = to_code(3, lambda d: numer_c.at[me_c], numer_c.at[me_c])
     for k in range(patients):
-        polar[k] = iterates[k]
-        value = mm(iterates[k], products[k], 1, 1)
-        projected[k] = value
-        term = value * mine[k]
-        total = term if total is None else total + term
-    numer[...] = total
-
-
-def numer_kernel(n_pat, n_code, numer, result, pat_all, code_all, mid, send_p, recv_p, send_c, recv_c):
-    me_p, me_c = lax.axis_index("pat"), lax.axis_index("code")
-    greet(n_pat, n_code, me_p, me_c)
-    copies = []
-    for d in range(1, n_pat):
-        copies.append(
-            remote(numer, pat_all.at[me_p], send_p.at[d], recv_p.at[d], (lax.rem(me_p + d, n_pat), me_c))
-        )
-    pat_all[me_p] = numer[...]
-    for copy in copies:
-        copy.wait_recv()
-    mid[...] = jnp.sum(pat_all[...], axis=0)
-    more = []
-    for d in range(1, n_code):
-        more.append(
-            remote(mid, code_all.at[me_c], send_c.at[d], recv_c.at[d], (me_p, lax.rem(me_c + d, n_code)))
-        )
-    code_all[me_c] = mid[...]
-    for copy in more:
-        copy.wait_recv()
-    result[...] = jnp.sum(code_all[...], axis=0)
-    for copy in copies + more:
-        copy.wait_send()
-
-
-def weight_kernel(numer, inverse, code_gram, polar, projected, mix_out, mix_gram, weight_out, spread):
-    patients, rank, visits = polar.shape
-    tile_rows = visits // VBLOCKS
-    mix = mm(numer[...], inverse[...])
+        for b in range(VBLOCKS):
+            piece = polars[k][:, b * tile_rows : (b + 1) * tile_rows]
+            polar_all[me_c, k * VBLOCKS + b] = piece.astype(bf16)
+    polar_c = to_code(4, lambda d: polar_all.at[me_c], polar_all.at[me_c])
+    for copy in numer_z:
+        copy.wait_recv()
+    mid[...] = jnp.sum(numer_c[...], axis=0)
+    numer_x = to_pat(2, mid, numer_p.at[me_p])
+    numer_p[me_p] = mid[...]
+    for copy in numer_x:
+        copy.wait_recv()
+    packed = jnp.sum(numer_p[...], axis=0)
+    numer = jnp.concatenate([packed[:, :rank], packed[:, rank:]], axis=0)
+
+    mix = mm(numer, first)
     mix_out[...] = mix
     square = mm(mix, mix, 0, 0)
-    mix_gram[...] = square
-    second = damped_inverse(square * code_gram[...])
-    terms = jnp.concatenate(
-        [jnp.sum(mix * projected[k], axis=0, keepdims=True) for k in range(patients)], axis=0
-    )
-    weight = jnp.maximum(mm(terms, second), 0.0)
-    weight_out[...] = weight
-    for k in range(patients):
-        value = mm(mix * weight[k : k + 1, :], polar[k], 0, 0).astype(bf16)
-        for b in range(VBLOCKS):
-            spread[k * VBLOCKS + b] = value[:, b * tile_rows : (b + 1) * tile_rows]
-
-
-def spread_kernel(
-    n_pat, n_code, spread, weight, mix_gram, spread_all, inverse, weight_all, row, send_c, recv_c, send_p, recv_p, here
-):
-    me_p, me_c = lax.axis_index("pat"), lax.axis_index("code")
-    greet(n_pat, n_code, me_p, me_c)
-    first, bulk = [], []
-    for d in range(1, n_code):
-        where = (me_p, lax.rem(me_c + d, n_code))
-        first.append(remote(weight, row.at[me_c], send_c.at[0, d], recv_c.at[0, d], where))
-    for d in range(n_code - 1, 0, -1):
-        where = (me_p, lax.rem(me_c + d, n_code))
-        bulk.append(remote(spread, spread_all.at[me_c], send_c.at[1, d], recv_c.at[1, d], where))
-    local = pltpu.make_async_copy(spread, spread_all.at[me_c], here.at[0])
-    local.start()
-    row[me_c] = weight[...]
-    for copy in first:
-        copy.wait_recv()
-    second = []
-    for d in range(1, n_pat):
-        second.append(
-            remote(row, weight_all.at[me_p], send_p.at[d], recv_p.at[d], (lax.rem(me_p + d, n_pat), me_c))
-        )
+    terms = jnp.concatenate([jnp.sum(mix * projected[k], axis=0, keepdims=True) for k in range(patients)], axis=0)
+    fresh = jnp.maximum(mm(terms, damped_inverse(square * code_gram)), 0.0)
+    weight_out[...] = fresh
+    row[me_c] = fresh
+    row_c = to_code(5, lambda d: row.at[me_c], row.at[me_c])
+    for copy in row_c:
+        copy.wait_recv()
+    row_p = to_pat(3, row, weight_all.at[me_p])
     weight_all[me_p] = row[...]
-    for copy in second:
+    for copy in polar_c:
+        copy.wait_recv()
+    for c in range(n_code):
+        for k in range(patients):
+            scaled = mix * row[c, k : k + 1, :]
+            high = scaled.astype(bf16)
+            left = jnp.concatenate([high, (scaled - high.astype(f32)).astype(bf16)], axis=0)
+            for b in range(VBLOCKS):
+                s = k * VBLOCKS + b
+                part = polar_all[c, s]
+                spread[c * own + s] = bmm(left, jnp.concatenate([part, part], axis=0), 0, 0).astype(bf16)
+    for copy in row_p:
         copy.wait_recv()
     rows = jnp.concatenate(
         [jnp.concatenate([weight_all[p, c] for c in range(n_code)], axis=0) for p in range(n_pat)], axis=0
     )
-    inverse[...] = damped_inverse(mix_gram[...] * mm(rows, rows, 0, 0))
-    for copy in bulk:
-        copy.wait_recv()
-    local.wait()
-    for copy in first + second + bulk:
+    inverse[...] = damped_inverse(square * mm(rows, rows, 0, 0))
+    for copy in gram_c + col_c + dev_c + old_p + gram_p + numer_z + polar_c + numer_x + row_c + row_p:
         copy.wait_send()
 
 
-def code_kernel(list_ref, count_ref, visits_ref, tiles, spread, acc):
+def code_kernel(list_ref, count_ref, visits_ref, tiles, spread, mix, weight, acc, mix_out, weight_out):
+    mix_out[...] = mix[...]
+    weight_out[...] = weight[...]
     slots, tile_rows, tile_cols = tiles.shape
     rank, codes = acc.shape
     acc[...] = jnp.zeros_like(acc)
@@ -512,59 +518,32 @@
         [pltpu.VMEM((2 * rank, codes), bf16), pltpu.VMEM((segments, rank, tile_rows), f32)],
         smem=3,
     )(listing, count, visit_counts, tiles, code_factor_t)
-    dev_all, col_all, gram_all, weight_all = call(
-        functools.partial(exchange_kernel, n_pat, n_code),
+    square = ((rank, rank), f32)
+    fresh = ((pat_own, rank), f32)
+    spread, second, mix_kept, weight_kept = call(
+        functools.partial(core_kernel, n_pat, n_code),
+        [((segments, rank, tile_rows), bf16), square, square, fresh],
+        5,
         [
-            ((n_code, own, rank, tile_rows), bf16),
-            ((n_code, own, tile_rows), f32),
-            ((n_pat, n_code, rank // n_pat, 2 * rank), f32),
-            ((n_pat, pat_row, rank), f32),
+            pltpu.VMEM((n_code, own, rank, tile_rows), bf16),
+            pltpu.VMEM((n_code, own, tile_rows), f32),
+            pltpu.VMEM((n_pat, n_code, rank // n_pat, 2 * rank), f32),
+            pltpu.VMEM((n_pat, pat_row, rank), f32),
+            pltpu.VMEM((n_code, rank // 2, 2 * rank), f32),
+            pltpu.VMEM((n_pat, rank // 2, 2 * rank), f32),
+            pltpu.VMEM((rank // 2, 2 * rank), f32),
+            pltpu.VMEM((n_code, own, rank, tile_rows), bf16),
+            pltpu.VMEM((n_code, pat_own, rank), f32),
+            pltpu.VMEM((n_pat, n_code, pat_own, rank), f32),
+            dma(6, n_code),
+            dma(6, n_code),
+            dma(4, n_pat),
+            dma(4, n_pat),
         ],
-        4,
-        [dma(3, n_code), dma(3, n_code), dma(2, n_pat), dma(2, n_pat), dma(4)],
         remote_id=1,
-    )(dev, col, gram, patient_weight)
-    square = ((rank, rank), f32)
-    polar, projected, numer, inverse, code_gram = call(
-        polar_kernel,
-        [((pat_own, rank, VBLOCKS * tile_rows), f32), ((pat_own, rank, rank), f32), square, square, square],
-        5,
-    )(dev_all, col_all, gram_all, weight_all, visit_mix)
-    (numer_sum,) = call(
-        functools.partial(numer_kernel, n_pat, n_code),
-        [square],
-        1,
-        [
-            pltpu.VMEM((n_pat, rank, rank), f32),
-            pltpu.VMEM((n_code, rank, rank), f32),
-            pltpu.VMEM((rank, rank), f32),
-            dma(n_pat),
-            dma(n_pat),
-            dma(n_code),
-            dma(n_code),
-        ],
-        remote_id=2,
-    )(numer)
-    mix_new, mix_gram, weight_new, spread = call(
-        weight_kernel, [square, square, ((pat_own, rank), f32), ((own, rank, tile_rows), bf16)], 5
-    )(numer_sum, inverse, code_gram, polar, projected)
-    spread_all, second = call(
-        functools.partial(spread_kernel, n_pat, n_code),
-        [((n_code, own, rank, tile_rows), bf16), square],
-        3,
-        [
-            pltpu.VMEM((n_pat, n_code, pat_own, rank), f32),
-            pltpu.VMEM((n_code, pat_own, rank), f32),
-            dma(2, n_code),
-            dma(2, n_code),
-            dma(n_pat),
-            dma(n_pat),
-            dma(1),
-        ],
-        remote_id=3,
-    )(spread, weight_new, mix_gram)
-    (code_numer,) = call(code_kernel, [((rank, codes), f32)], 5, smem=3)(
-        listing, count, visit_counts, tiles, spread_all.reshape(segments, rank, tile_rows)
+    )(dev, col, gram, patient_weight, visit_mix)
+    code_numer, mix_new, weight_new = call(code_kernel, [((rank, codes), f32), square, fresh], 7, smem=3)(
+        listing, count, visit_counts, tiles, spread, mix_kept, weight_kept
     )
     if chips == 4:
         (code_new,) = call(

time: 95.4 us -> 84.1 us (0.88)
  Pallas kernels: 85.6 us -> 75.1 us
    pallas_call x6 -> x2, Pallas kernels: 57.5 us -> 46.7 us  [the longest x1 44.9 us: body(): call(functools.partial(core_kernel, n_pat, n_code), [((segments, rank, ti...]
    unnamed x20 -> x14, local copies, waits for them, and re-layouts: 5.81 us -> 5.12 us
where the time goes in v2:
time: 84.1 us; the launch traced here: 83.9 us
  Pallas kernels  75.1 us (89%)
  local copies, waits for them, and re-layouts  5.12 us (6%)
  other arithmetic  2.29 us (3%)
  between operations  1.35 us (2%)
    pallas_call x1, Pallas kernels, body(): call(functools.partial(core_kernel, n_pat, n_code), [((segments, rank, ti...  44.9 us
    pallas_call x1, Pallas kernels, body(): call(functools.partial(quad_kernel, n_pat), [((rank, codes), bf16)], 2, [...  25.1 us
    unnamed x14, local copies, waits for them, and re-layouts  5.12 us
    pallas_call x1, Pallas kernels, body(): call(products_kernel, [((segments, rank, tile_rows), bf16), ((segments, t...  3.36 us
    convert_element_type x1, other arithmetic, body(): return (code_new.astype(f32), mix_new, weight_new)  2.29 us
    pallas_call x1, Pallas kernels, body(): call(code_kernel, [((rank, codes), f32), square, fresh], 7, smem=3)  1.81 us

profile of v2, /device:TPU:0, one launch (start us, length us, event | category | flops | bytes accessed | tf_op | source)
XLA Modules:
  0.0 83.9 jit_solution(16899971510207418517)
XLA Ops:
  0.6 0.0 copy-start.4
  1.3 0.0 copy-start
  1.3 1.6 %copy-done = bf16[1,1,16,128,512]{4,3,2,1,0:T(8,128)(2,1)S(1)} copy-done((bf16[1,1,16,128,512]{4,3,2,1,0:T(8,128)(2,1)S(1)}, bf16[1,1,16,128,512]{4,3,2,1,0:T(8,128)(2,1)}, u32[]{:S(2)}) %copy-start) | copy-done | bytes 2097176
  2.9 0.0 copy-start.2
  2.9 2.2 %copy-done.2 = f32[64,16384]{1,0:T(8,128)S(1)} copy-done((f32[64,16384]{1,0:T(8,128)S(1)}, f32[64,16384]{1,0:T(8,128)}, u32[]{:S(2)}) %copy-start.2) | copy-done | bytes 4194328
  5.1 0.0 copy-start.5
  5.1 0.7 copy-done.5
  5.8 0.0 copy-start.6
  5.8 0.7 copy-done.6
  6.4 0.0 copy-start.3
  6.4 0.0 copy-start.1
  6.4 3.4 %shard_map.94 = (bf16[32,64,128]{2,1,0:T(8,128)(2,1)S(1)}, f32[32,128]{1,0:T(8,128)S(1)}, f32[8,8,128]{2,1,0:T(8,128)S(1)}) custom-call(s32[3,1,16]{2,1,0:T(1,128)S(1)} %bitcast.7, s32[1]{0:T(128)} %bitcast.3.count_ref, s32[16]{0:T(128)S(1)} %copy-done.6, bf16[16,128,512]{2,1,0:T(8,128)(2,1)S(1)} %bitcast.5, f32[64,16384]{1,0:T(8,128)S(1)} %copy-done.2), custom_call_target="tpu_custom_call" | custom-call | tf_op jit(solution)/shard_map/pallas_call | solution.py:514
  9.8 0.0 copy-done.4
  9.8 0.0 copy-done.3
  9.8 44.9 %shard_map.95 = (bf16[32,64,128]{2,1,0:T(8,128)(2,1)S(1)}, f32[64,64]{1,0:T(8,128)S(1)}, f32[64,64]{1,0:T(8,128)S(1)}, f32[4,64]{1,0:T(4,128)S(1)}) custom-call(bf16[32,64,128]{2,1,0:T(8,128)(2,1)S(1)} %get-tuple-element.13.dev, f32[32,128]{1,0:T(8,128)S(1)} %get-tuple-element.14.col, f32[8,8,128]{2,1,0:T(8,128)S(1)} %get-tuple-element.15.gram, ...), custom_call_target="tpu_custom_call" | custom-call | tf_op jit(solution)/shard_map/pallas_call | solution.py:523
  54.7 0.0 copy-done.1
  54.7 1.8 %shard_map.96 = (f32[64,16384]{1,0:T(8,128)S(1)}, f32[64,64]{1,0:T(8,128)}, f32[4,64]{1,0:T(4,128)}) custom-call(s32[3,1,16]{2,1,0:T(1,128)S(1)} %bitcast.8, s32[1]{0:T(128)} %bitcast.4.count_ref, s32[16]{0:T(128)S(1)} %copy-done.6, bf16[16,128,512]{2,1,0:T(8,128)(2,1)S(1)} %bitcast.6, bf16[32,64,128]{2,1,0:T(8,128)(2,1)S(1)} %get-tuple-element.16.spread, ...), custom_call_target="tpu_custom_call" | custom-call | tf_op jit(solution)/shard_map/pallas_call | solution.py:545
  56.5 25.1 %shard_map.97 = bf16[64,16384]{1,0:T(8,128)(2,1)S(1)} custom-call(f32[64,16384]{1,0:T(8,128)S(1)} %get-tuple-element.19.numer, f32[64,64]{1,0:T(8,128)S(1)} %get-tuple-element.20.inverse), custom_call_target="tpu_custom_call" | custom-call | tf_op jit(solution)/shard_map/pallas_call | solution.py:549
  81.6 2.3 %convert_element_type.3 = f32[64,16384]{1,0:T(8,128)} convert(bf16[64,16384]{1,0:T(8,128)(2,1)S(1)} %shard_map.97) | non-fusion elementwise | flops 1048576 | bytes 6291456 | tf_op jit(solution)/shard_map/convert_element_type | solution.py:576
Async XLA Ops:
  0.6 9.2 %copy-start.4 = (f32[16,64]{1,0:T(8,128)S(1)}, f32[16,64]{1,0:T(8,128)}, u32[]{:S(2)}) copy-start(f32[16,64]{1,0:T(8,128)} %weight.1) | copy-start | bytes 12292
  1.3 1.6 %copy-start = (bf16[1,1,16,128,512]{4,3,2,1,0:T(8,128)(2,1)S(1)}, bf16[1,1,16,128,512]{4,3,2,1,0:T(8,128)(2,1)}, u32[]{:S(2)}) copy-start(bf16[1,1,16,128,512]{4,3,2,1,0:T(8,128)(2,1)} %param.7) | copy-start | bytes 6291460
  2.9 2.2 %copy-start.2 = (f32[64,16384]{1,0:T(8,128)S(1)}, f32[64,16384]{1,0:T(8,128)}, u32[]{:S(2)}) copy-start(f32[64,16384]{1,0:T(8,128)} %factor.1) | copy-start | bytes 12582916
  5.1 0.7 copy-start.5
  5.8 0.7 copy-start.6
  6.4 3.4 %copy-start.3 = (f32[64,64]{1,0:T(8,128)S(1)}, f32[64,64]{1,0:T(8,128)}, u32[]{:S(2)}) copy-start(f32[64,64]{1,0:T(8,128)} %mix_in.1) | copy-start | bytes 49156
  6.4 48.3 %copy-start.1 = (bf16[1,1,16,128,512]{4,3,2,1,0:T(8,128)(2,1)S(1)}, bf16[1,1,16,128,512]{4,3,2,1,0:T(8,128)(2,1)}, u32[]{:S(2)}) copy-start(bf16[1,1,16,128,512]{4,3,2,1,0:T(8,128)(2,1)} %param.7) | copy-start | bytes 6291460

commit v3 on v2

--- a/solution.py
+++ b/solution.py
@@ -9,7 +9,8 @@
 
 VBLOCKS = 2
 NS_STEPS = 8
-INVERSE_STEPS = 8
+INVERSE_STEPS = 7
+STREAMS = 2
 MESH = pl.DeviceIdType.MESH
 damping = 0.1
 epsilon = 1e-06
@@ -331,16 +332,13 @@
     core, chip = lax.rem(me_p, 2), me_p // 2
     at_x, at_y = lax.rem(chip, 2), chip // 2
     width = numer.shape[1] // n_pat
-    part = width // 2
+    span = width // STREAMS
+    part = span // 2
     chips = [chip, at_y * 2 + 1 - at_x, (1 - at_y) * 2 + at_x, (1 - at_y) * 2 + 1 - at_x]
     partner = (chip * 2 + 1 - core, me_c)
     along_x, along_y = (chips[1] * 2 + core, me_c), (chips[2] * 2 + core, me_c)
-    copies = []
-
-    def lanes(index, half=None):
-        if half is None:
-            return pl.ds(pl.multiple_of(index * width, width), width)
-        return pl.ds(pl.multiple_of(index * width + half * part, part), part)
+    copies, tail = [], []
+    order = (3, 1, 2, 0)
 
     def go(src, dst, where):
         n = len(copies)
@@ -350,71 +348,86 @@
     barrier = pltpu.get_barrier_semaphore()
     for where in (partner, along_x, along_y):
         pl.semaphore_signal(barrier, inc=1, device_id=where, device_id_type=MESH)
-    pl.semaphore_wait(barrier, 3)
-
     left = stacked_inverse(inverse[...])
-    order = (3, 1, 2, 0)
-    pairs = {}
-    for s in order:
-        give[s] = solved_block(left, numer[:, lanes(chips[s] * 2 + 1 - core)]).astype(bf16)
-        pairs[s] = go(give.at[s], pair.at[s], partner)
-    for s in order:
-        keep[s] = solved_block(left, numer[:, lanes(chips[s] * 2 + core)])
-    for s in order:
-        pairs[s].wait_recv()
-        keep[s] += pair[s].astype(f32)
-        if s == 3:
-            send_x[0] = keep[3, :, :part].astype(bf16)
-            x_far = go(send_x.at[0], got_x.at[0], along_x)
-            send_y[0] = keep[3, :, part:].astype(bf16)
-            y_far = go(send_y.at[0], got_y.at[0], along_y)
-        elif s == 1:
-            send_x[1] = keep[1, :, :part].astype(bf16)
-            x_near = go(send_x.at[1], got_x.at[1], along_x)
-        elif s == 2:
-            send_y[1] = keep[2, :, part:].astype(bf16)
-            y_near = go(send_y.at[1], got_y.at[1], along_y)
-    x_far.wait_recv()
-    send_y[2] = (keep[2, :, :part] + got_x[0].astype(f32)).astype(bf16)
-    y_last = go(send_y.at[2], got_y.at[2], along_y)
-    y_far.wait_recv()
-    send_x[2] = (keep[1, :, part:] + got_y[0].astype(f32)).astype(bf16)
-    x_last = go(send_x.at[2], got_x.at[2], along_x)
-    x_near.wait_recv()
-    y_last.wait_recv()
-    low = keep[0, :, :part] + got_x[1].astype(f32) + got_y[2].astype(f32)
-    fin[0] = jnp.maximum(low, 0.0).astype(bf16)
-    spots = [out.at[:, lanes(me_p, h)] for h in range(2)]
-    x_low = go(fin.at[0], spots[0], along_x)
-    y_near.wait_recv()
-    x_last.wait_recv()
-    high = keep[0, :, part:] + got_y[1].astype(f32) + got_x[2].astype(f32)
-    fin[1] = jnp.maximum(high, 0.0).astype(bf16)
-    y_high = go(fin.at[1], spots[1], along_y)
-    x_high = go(fin.at[1], spots[1], along_x)
-    y_low = go(fin.at[0], spots[0], along_y)
-    tail = [go(fin.at[0], spots[0], partner), go(fin.at[1], spots[1], partner)]
-    out[:, lanes(me_p, 0)] = fin[0]
-    out[:, lanes(me_p, 1)] = fin[1]
-
-    def pass_on(s, half, where):
-        spot = out.at[:, lanes(chips[s] * 2 + core, half)]
-        return go(spot, spot, where)
-
-    x_low.wait_recv()
-    low_far = pass_on(1, 0, along_y)
-    tail.append(pass_on(1, 0, partner))
-    y_high.wait_recv()
-    high_far = pass_on(2, 1, along_x)
-    tail.append(pass_on(2, 1, partner))
-    x_high.wait_recv()
-    tail.append(pass_on(1, 1, partner))
-    y_low.wait_recv()
-    tail.append(pass_on(2, 0, partner))
-    low_far.wait_recv()
-    tail.append(pass_on(3, 0, partner))
-    high_far.wait_recv()
-    tail.append(pass_on(3, 1, partner))
+
+    def stream(g):
+        def lanes(index, half=None):
+            if half is None:
+                return pl.ds(pl.multiple_of(index * width + g * span, part), span)
+            return pl.ds(pl.multiple_of(index * width + g * span + half * part, part), part)
+
+        pairs = {}
+        for s in order:
+            give[g, s] = solved_block(left, numer[:, lanes(chips[s] * 2 + 1 - core)]).astype(bf16)
+            if g == 0 and s == order[0]:
+                pl.semaphore_wait(barrier, 3)
+            pairs[s] = go(give.at[g, s], pair.at[g, s], partner)
+        yield
+        for s in order:
+            keep[g, s] = solved_block(left, numer[:, lanes(chips[s] * 2 + core)])
+            pairs[s].wait_recv()
+            keep[g, s] += pair[g, s].astype(f32)
+            if s == 3:
+                send_x[g, 0] = keep[g, 3, :, :part].astype(bf16)
+                x_far = go(send_x.at[g, 0], got_x.at[g, 0], along_x)
+                send_y[g, 0] = keep[g, 3, :, part:].astype(bf16)
+                y_far = go(send_y.at[g, 0], got_y.at[g, 0], along_y)
+            elif s == 1:
+                send_x[g, 1] = keep[g, 1, :, :part].astype(bf16)
+                x_near = go(send_x.at[g, 1], got_x.at[g, 1], along_x)
+            elif s == 2:
+                send_y[g, 1] = keep[g, 2, :, part:].astype(bf16)
+                y_near = go(send_y.at[g, 1], got_y.at[g, 1], along_y)
+        yield
+        x_far.wait_recv()
+        send_y[g, 2] = (keep[g, 2, :, :part] + got_x[g, 0].astype(f32)).astype(bf16)
+        y_last = go(send_y.at[g, 2], got_y.at[g, 2], along_y)
+        y_far.wait_recv()
+        send_x[g, 2] = (keep[g, 1, :, part:] + got_y[g, 0].astype(f32)).astype(bf16)
+        x_last = go(send_x.at[g, 2], got_x.at[g, 2], along_x)
+        yield
+        x_near.wait_recv()
+        y_last.wait_recv()
+        low = keep[g, 0, :, :part] + got_x[g, 1].astype(f32) + got_y[g, 2].astype(f32)
+        fin[g, 0] = jnp.maximum(low, 0.0).astype(bf16)
+        spots = [out.at[:, lanes(me_p, h)] for h in range(2)]
+        x_low = go(fin.at[g, 0], spots[0], along_x)
+        y_near.wait_recv()
+        x_last.wait_recv()
+        high = keep[g, 0, :, part:] + got_y[g, 1].astype(f32) + got_x[g, 2].astype(f32)
+        fin[g, 1] = jnp.maximum(high, 0.0).astype(bf16)
+        y_high = go(fin.at[g, 1], spots[1], along_y)
+        x_high = go(fin.at[g, 1], spots[1], along_x)
+        y_low = go(fin.at[g, 0], spots[0], along_y)
+        tail.append(go(fin.at[g, 0], spots[0], partner))
+        tail.append(go(fin.at[g, 1], spots[1], partner))
+        out[:, lanes(me_p, 0)] = fin[g, 0]
+        out[:, lanes(me_p, 1)] = fin[g, 1]
+        yield
+
+        def pass_on(s, half, where):
+            spot = out.at[:, lanes(chips[s] * 2 + core, half)]
+            return go(spot, spot, where)
+
+        x_low.wait_recv()
+        low_far = pass_on(1, 0, along_y)
+        tail.append(pass_on(1, 0, partner))
+        y_high.wait_recv()
+        high_far = pass_on(2, 1, along_x)
+        tail.append(pass_on(2, 1, partner))
+        x_high.wait_recv()
+        tail.append(pass_on(1, 1, partner))
+        y_low.wait_recv()
+        tail.append(pass_on(2, 0, partner))
+        yield
+        low_far.wait_recv()
+        tail.append(pass_on(3, 0, partner))
+        high_far.wait_recv()
+        tail.append(pass_on(3, 1, partner))
+        yield
+
+    for _ in zip(*[stream(g) for g in range(STREAMS)]):
+        pass
     for copy in tail:
         copy.wait_recv()
     for copy in copies:
@@ -546,21 +559,22 @@
         listing, count, visit_counts, tiles, spread, mix_kept, weight_kept
     )
     if chips == 4:
+        span = width // STREAMS
         (code_new,) = call(
             functools.partial(quad_kernel, n_pat),
             [((rank, codes), bf16)],
             2,
             [
-                pltpu.VMEM((chips, rank, width), bf16),
-                pltpu.VMEM((chips, rank, width), f32),
-                pltpu.VMEM((chips, rank, width), bf16),
-                pltpu.VMEM((3, rank, width // 2), bf16),
-                pltpu.VMEM((3, rank, width // 2), bf16),
-                pltpu.VMEM((3, rank, width // 2), bf16),
-                pltpu.VMEM((3, rank, width // 2), bf16),
-                pltpu.VMEM((2, rank, width // 2), bf16),
-                dma(24),
-                dma(24),
+                pltpu.VMEM((STREAMS, chips, rank, span), bf16),
+                pltpu.VMEM((STREAMS, chips, rank, span), f32),
+                pltpu.VMEM((STREAMS, chips, rank, span), bf16),
+                pltpu.VMEM((STREAMS, 3, rank, span // 2), bf16),
+                pltpu.VMEM((STREAMS, 3, rank, span // 2), bf16),
+                pltpu.VMEM((STREAMS, 3, rank, span // 2), bf16),
+                pltpu.VMEM((STREAMS, 3, rank, span // 2), bf16),
+                pltpu.VMEM((STREAMS, 2, rank, span // 2), bf16),
+                dma(24 * STREAMS),
+                dma(24 * STREAMS),
             ],
             remote_id=4,
         )(code_numer, second)

time: 84.1 us -> 82.9 us (0.986)
  Pallas kernels: 75.1 us -> 73.9 us
where the time goes in v3:
time: 82.9 us; the launch traced here: 82.7 us
  Pallas kernels  73.9 us (89%)
  local copies, waits for them, and re-layouts  5.12 us (6%)
  other arithmetic  2.29 us (3%)
  between operations  1.35 us (2%)
    pallas_call x1, Pallas kernels, body(): call(functools.partial(core_kernel, n_pat, n_code), [((segments, rank, ti...  44.3 us
    pallas_call x1, Pallas kernels, body(): call(functools.partial(quad_kernel, n_pat), [((rank, codes), bf16)], 2, [...  24.5 us
    unnamed x14, local copies, waits for them, and re-layouts  5.12 us
    pallas_call x1, Pallas kernels, body(): call(products_kernel, [((segments, rank, tile_rows), bf16), ((segments, t...  3.36 us
    convert_element_type x1, other arithmetic, body(): return (code_new.astype(f32), mix_new, weight_new)  2.29 us
    pallas_call x1, Pallas kernels, body(): call(code_kernel, [((rank, codes), f32), square, fresh], 7, smem=3)  1.81 us

profile of v3, /device:TPU:0, one launch (start us, length us, event | category | flops | bytes accessed | tf_op | source)
XLA Modules:
  0.0 82.7 jit_solution(11071087817151875449)
XLA Ops:
  0.6 0.0 copy-start.4
  1.3 0.0 copy-start
  1.3 1.6 %copy-done = bf16[1,1,16,128,512]{4,3,2,1,0:T(8,128)(2,1)S(1)} copy-done((bf16[1,1,16,128,512]{4,3,2,1,0:T(8,128)(2,1)S(1)}, bf16[1,1,16,128,512]{4,3,2,1,0:T(8,128)(2,1)}, u32[]{:S(2)}) %copy-start) | copy-done | bytes 2097176
  2.9 0.0 copy-start.2
  2.9 2.2 %copy-done.2 = f32[64,16384]{1,0:T(8,128)S(1)} copy-done((f32[64,16384]{1,0:T(8,128)S(1)}, f32[64,16384]{1,0:T(8,128)}, u32[]{:S(2)}) %copy-start.2) | copy-done | bytes 4194328
  5.1 0.0 copy-start.5
  5.1 0.7 copy-done.5
  5.8 0.0 copy-start.6
  5.8 0.7 copy-done.6
  6.4 0.0 copy-start.3
  6.4 0.0 copy-start.1
  6.4 3.4 %shard_map.94 = (bf16[32,64,128]{2,1,0:T(8,128)(2,1)S(1)}, f32[32,128]{1,0:T(8,128)S(1)}, f32[8,8,128]{2,1,0:T(8,128)S(1)}) custom-call(s32[3,1,16]{2,1,0:T(1,128)S(1)} %bitcast.7, s32[1]{0:T(128)} %bitcast.3.count_ref, s32[16]{0:T(128)S(1)} %copy-done.6, bf16[16,128,512]{2,1,0:T(8,128)(2,1)S(1)} %bitcast.5, f32[64,16384]{1,0:T(8,128)S(1)} %copy-done.2), custom_call_target="tpu_custom_call" | custom-call | tf_op jit(solution)/shard_map/pallas_call | solution.py:527
  9.8 0.0 copy-done.4
  9.8 0.0 copy-done.3
  9.8 44.3 %shard_map.95 = (bf16[32,64,128]{2,1,0:T(8,128)(2,1)S(1)}, f32[64,64]{1,0:T(8,128)S(1)}, f32[64,64]{1,0:T(8,128)S(1)}, f32[4,64]{1,0:T(4,128)S(1)}) custom-call(bf16[32,64,128]{2,1,0:T(8,128)(2,1)S(1)} %get-tuple-element.13.dev, f32[32,128]{1,0:T(8,128)S(1)} %get-tuple-element.14.col, f32[8,8,128]{2,1,0:T(8,128)S(1)} %get-tuple-element.15.gram, ...), custom_call_target="tpu_custom_call" | custom-call | tf_op jit(solution)/shard_map/pallas_call | solution.py:536
  54.1 0.0 copy-done.1
  54.1 1.8 %shard_map.96 = (f32[64,16384]{1,0:T(8,128)S(1)}, f32[64,64]{1,0:T(8,128)}, f32[4,64]{1,0:T(4,128)}) custom-call(s32[3,1,16]{2,1,0:T(1,128)S(1)} %bitcast.8, s32[1]{0:T(128)} %bitcast.4.count_ref, s32[16]{0:T(128)S(1)} %copy-done.6, bf16[16,128,512]{2,1,0:T(8,128)(2,1)S(1)} %bitcast.6, bf16[32,64,128]{2,1,0:T(8,128)(2,1)S(1)} %get-tuple-element.16.spread, ...), custom_call_target="tpu_custom_call" | custom-call | tf_op jit(solution)/shard_map/pallas_call | solution.py:558
  55.9 24.5 %shard_map.97 = bf16[64,16384]{1,0:T(8,128)(2,1)S(1)} custom-call(f32[64,16384]{1,0:T(8,128)S(1)} %get-tuple-element.19.numer, f32[64,64]{1,0:T(8,128)S(1)} %get-tuple-element.20.inverse), custom_call_target="tpu_custom_call" | custom-call | tf_op jit(solution)/shard_map/pallas_call | solution.py:563
  80.4 2.3 %convert_element_type.3 = f32[64,16384]{1,0:T(8,128)} convert(bf16[64,16384]{1,0:T(8,128)(2,1)S(1)} %shard_map.97) | non-fusion elementwise | flops 1048576 | bytes 6291456 | tf_op jit(solution)/shard_map/convert_element_type | solution.py:590
Async XLA Ops:
  0.6 9.2 %copy-start.4 = (f32[16,64]{1,0:T(8,128)S(1)}, f32[16,64]{1,0:T(8,128)}, u32[]{:S(2)}) copy-start(f32[16,64]{1,0:T(8,128)} %weight.1) | copy-start | bytes 12292
  1.3 1.6 %copy-start = (bf16[1,1,16,128,512]{4,3,2,1,0:T(8,128)(2,1)S(1)}, bf16[1,1,16,128,512]{4,3,2,1,0:T(8,128)(2,1)}, u32[]{:S(2)}) copy-start(bf16[1,1,16,128,512]{4,3,2,1,0:T(8,128)(2,1)} %param.7) | copy-start | bytes 6291460
  2.9 2.2 %copy-start.2 = (f32[64,16384]{1,0:T(8,128)S(1)}, f32[64,16384]{1,0:T(8,128)}, u32[]{:S(2)}) copy-start(f32[64,16384]{1,0:T(8,128)} %factor.1) | copy-start | bytes 12582916
  5.1 0.7 copy-start.5
  5.8 0.7 copy-start.6
  6.4 3.4 %copy-start.3 = (f32[64,64]{1,0:T(8,128)S(1)}, f32[64,64]{1,0:T(8,128)}, u32[]{:S(2)}) copy-start(f32[64,64]{1,0:T(8,128)} %mix_in.1) | copy-start | bytes 49156
  6.4 47.7 %copy-start.1 = (bf16[1,1,16,128,512]{4,3,2,1,0:T(8,128)(2,1)S(1)}, bf16[1,1,16,128,512]{4,3,2,1,0:T(8,128)(2,1)}, u32[]{:S(2)}) copy-start(bf16[1,1,16,128,512]{4,3,2,1,0:T(8,128)(2,1)} %param.7) | copy-start | bytes 6291460

commit v4 on v3

--- a/solution.py
+++ b/solution.py
@@ -71,8 +71,7 @@
     return owner * VBLOCKS + block, code, limit
 
 
-def products_kernel(list_ref, count_ref, visits_ref, tiles, factor, dev, col, gram, split, acc):
-    slots, tile_rows, tile_cols = tiles.shape
+def gram_kernel(factor, high_out, gram, split):
     rank, codes = factor.shape
     step = min(2048, codes)
     total = jnp.zeros((2 * rank, 2 * rank), f32)
@@ -80,6 +79,7 @@
     for start in range(0, codes, step):
         part = factor[:, start : start + step]
         high = part.astype(bf16)
+        high_out[:, start : start + step] = high
         split[:rank, start : start + step] = high
         split[rank:, start : start + step] = (part - high.astype(f32)).astype(bf16)
         profile += jnp.sum(part, axis=1, keepdims=True)
@@ -91,11 +91,17 @@
     rows = gram.shape[1]
     for p in range(gram.shape[0]):
         gram[p] = both[p * rows : (p + 1) * rows, :]
+
+
+def products_kernel(list_ref, count_ref, visits_ref, tiles, factor, gram, dev, col, acc):
+    slots, tile_rows, tile_cols = tiles.shape
+    rank, codes = factor.shape
+    profile = jnp.concatenate([gram[p] for p in range(gram.shape[0])], axis=0)[:, rank : rank + 1]
     acc[...] = jnp.zeros_like(acc)
     lane_at = lax.broadcasted_iota(jnp.int32, (rank, tile_rows), 1)
     for slot in range(slots):
         segment, code, limit = live_rows(list_ref, count_ref, visits_ref, slot, tile_rows)
-        picked = split[:rank, pl.ds(pl.multiple_of(code * tile_cols, tile_cols), tile_cols)]
+        picked = factor[:, pl.ds(pl.multiple_of(code * tile_cols, tile_cols), tile_cols)]
         contrib = bmm(picked, tiles[slot], 1, 1)
         acc[segment] += jnp.where(lane_at < limit, contrib, 0.0)
     whole = 1.0 / jnp.sum(profile, axis=0, keepdims=True)
@@ -524,13 +530,19 @@
     chips = n_pat // 2
     width = codes // n_pat
 
-    dev, col, gram = call(
+    high, gram = call(
+        gram_kernel,
+        [((rank, codes), bf16), ((n_pat, rank // n_pat, 2 * rank), f32)],
+        1,
+        [pltpu.VMEM((2 * rank, codes), bf16)],
+    )(code_factor_t)
+    dev, col = call(
         products_kernel,
-        [((segments, rank, tile_rows), bf16), ((segments, tile_rows), f32), ((n_pat, rank // n_pat, 2 * rank), f32)],
-        5,
-        [pltpu.VMEM((2 * rank, codes), bf16), pltpu.VMEM((segments, rank, tile_rows), f32)],
+        [((segments, rank, tile_rows), bf16), ((segments, tile_rows), f32)],
+        6,
+        [pltpu.VMEM((segments, rank, tile_rows), f32)],
         smem=3,
-    )(listing, count, visit_counts, tiles, code_factor_t)
+    )(listing, count, visit_counts, tiles, high, gram)
     square = ((rank, rank), f32)
     fresh = ((pat_own, rank), f32)
     spread, second, mix_kept, weight_kept = call(

time: 82.9 us -> 79.7 us (0.961)
  local copies, waits for them, and re-layouts: 5.12 us -> 2.2 us
    unnamed x14 -> x12, local copies, waits for them, and re-layouts: 5.12 us -> 2.2 us
    pallas_call x1, Pallas kernels: 3.36 us -> 1.56 us  [body(): call(products_kernel, [((segments, rank, tile_rows), bf16), ((segments, t...]
    pallas_call x0 -> x1, Pallas kernels: none -> 1.42 us  [body(): call(gram_kernel, [((rank, codes), bf16), ((n_pat, rank // n_pat, 2 * ran...]
where the time goes in v4:
time: 79.7 us; the launch traced here: 79.6 us
  Pallas kernels  73.6 us (92%)
  other arithmetic  2.29 us (3%)
  local copies, waits for them, and re-layouts  2.2 us (3%)
  between operations  1.52 us (2%)
    pallas_call x1, Pallas kernels, body(): call(functools.partial(core_kernel, n_pat, n_code), [((segments, rank, ti...  44.3 us
    pallas_call x1, Pallas kernels, body(): call(functools.partial(quad_kernel, n_pat), [((rank, codes), bf16)], 2, [...  24.5 us
    convert_element_type x1, other arithmetic, body(): return (code_new.astype(f32), mix_new, weight_new)  2.29 us
    unnamed x12, local copies, waits for them, and re-layouts  2.2 us
    pallas_call x1, Pallas kernels, body(): call(code_kernel, [((rank, codes), f32), square, fresh], 7, smem=3)  1.83 us

profile of v4, /device:TPU:0, one launch (start us, length us, event | category | flops | bytes accessed | tf_op | source)
XLA Modules:
  0.0 79.6 jit_solution(14296559657383618321)
XLA Ops:
  0.6 0.0 copy-start
  1.4 0.0 copy-start.1
  1.4 2.2 %copy-done.1 = f32[64,16384]{1,0:T(8,128)S(1)} copy-done((f32[64,16384]{1,0:T(8,128)S(1)}, f32[64,16384]{1,0:T(8,128)}, u32[]{:S(2)}) %copy-start.1) | copy-done | bytes 4194328
  3.6 0.0 copy-start.4
  3.6 0.0 copy-start.5
  3.6 0.0 copy-start.2
  3.6 0.0 copy-start.3
  3.6 1.4 %shard_map.94 = (bf16[64,16384]{1,0:T(8,128)(2,1)S(1)}, f32[8,8,128]{2,1,0:T(8,128)S(1)}) custom-call(f32[64,16384]{1,0:T(8,128)S(1)} %copy-done.1), custom_call_target="tpu_custom_call" | custom-call | tf_op jit(solution)/shard_map/pallas_call | solution.py:533
  5.1 0.0 copy-done
  5.1 0.0 copy-done.4
  5.1 0.0 copy-done.5
  5.1 1.6 %shard_map.95 = (bf16[32,64,128]{2,1,0:T(8,128)(2,1)S(1)}, f32[32,128]{1,0:T(8,128)S(1)}) custom-call(s32[3,1,16]{2,1,0:T(1,128)S(1)} %bitcast.7, s32[1]{0:T(128)} %bitcast.3.count_ref, s32[16]{0:T(128)S(1)} %copy-done.5, bf16[16,128,512]{2,1,0:T(8,128)(2,1)S(1)} %bitcast.5, bf16[64,16384]{1,0:T(8,128)(2,1)S(1)} %get-tuple-element.14.factor, ...), custom_call_target="tpu_custom_call" | custom-call | tf_op jit(solution)/shard_map/pallas_call | solution.py:539
  6.7 0.0 copy-done.2
  6.7 0.0 copy-done.3
  6.7 44.3 %shard_map.96 = (bf16[32,64,128]{2,1,0:T(8,128)(2,1)S(1)}, f32[64,64]{1,0:T(8,128)S(1)}, f32[64,64]{1,0:T(8,128)S(1)}, f32[4,64]{1,0:T(4,128)S(1)}) custom-call(bf16[32,64,128]{2,1,0:T(8,128)(2,1)S(1)} %get-tuple-element.16.dev, f32[32,128]{1,0:T(8,128)S(1)} %get-tuple-element.17.col, f32[8,8,128]{2,1,0:T(8,128)S(1)} %get-tuple-element.15.gram, ...), custom_call_target="tpu_custom_call" | custom-call | tf_op jit(solution)/shard_map/pallas_call | solution.py:548
  51.0 1.8 %shard_map.97 = (f32[64,16384]{1,0:T(8,128)S(1)}, f32[64,64]{1,0:T(8,128)}, f32[4,64]{1,0:T(4,128)}) custom-call(s32[3,1,16]{2,1,0:T(1,128)S(1)} %bitcast.8, s32[1]{0:T(128)} %bitcast.4.count_ref, s32[16]{0:T(128)S(1)} %copy-done.5, bf16[16,128,512]{2,1,0:T(8,128)(2,1)S(1)} %bitcast.6, bf16[32,64,128]{2,1,0:T(8,128)(2,1)S(1)} %get-tuple-element.18.spread, ...), custom_call_target="tpu_custom_call" | custom-call | tf_op jit(solution)/shard_map/pallas_call | solution.py:570
  52.8 24.5 %shard_map.98 = bf16[64,16384]{1,0:T(8,128)(2,1)S(1)} custom-call(f32[64,16384]{1,0:T(8,128)S(1)} %get-tuple-element.21.numer, f32[64,64]{1,0:T(8,128)S(1)} %get-tuple-element.22.inverse), custom_call_target="tpu_custom_call" | custom-call | tf_op jit(solution)/shard_map/pallas_call | solution.py:575
  77.3 2.3 %convert_element_type.3 = f32[64,16384]{1,0:T(8,128)} convert(bf16[64,16384]{1,0:T(8,128)(2,1)S(1)} %shard_map.98) | non-fusion elementwise | flops 1048576 | bytes 6291456 | tf_op jit(solution)/shard_map/convert_element_type | solution.py:602
Async XLA Ops:
  0.6 4.4 %copy-start = (bf16[1,1,16,128,512]{4,3,2,1,0:T(8,128)(2,1)S(1)}, bf16[1,1,16,128,512]{4,3,2,1,0:T(8,128)(2,1)}, u32[]{:S(2)}) copy-start(bf16[1,1,16,128,512]{4,3,2,1,0:T(8,128)(2,1)} %param.7) | copy-start | bytes 6291460
  1.4 2.2 %copy-start.1 = (f32[64,16384]{1,0:T(8,128)S(1)}, f32[64,16384]{1,0:T(8,128)}, u32[]{:S(2)}) copy-start(f32[64,16384]{1,0:T(8,128)} %factor.1) | copy-start | bytes 12582916
  3.6 1.4 %copy-start.4 = (s32[1,1,3,16]{3,1,2,0:T(1,128)S(1)}, s32[1,1,3,16]{3,1,2,0:T(1,128)}, u32[]{:S(2)}) copy-start(s32[1,1,3,16]{3,1,2,0:T(1,128)} %param.8) | copy-start | bytes 580
  3.6 1.5 %copy-start.5 = (s32[16]{0:T(128)S(1)}, s32[16]{0:T(128)}, u32[]{:S(2)}) copy-start(s32[16]{0:T(128)} %visits_ref.3) | copy-start | bytes 196
  3.6 3.0 %copy-start.2 = (f32[64,64]{1,0:T(8,128)S(1)}, f32[64,64]{1,0:T(8,128)}, u32[]{:S(2)}) copy-start(f32[64,64]{1,0:T(8,128)} %mix_in.1) | copy-start | bytes 49156
  3.6 3.0 %copy-start.3 = (f32[16,64]{1,0:T(8,128)S(1)}, f32[16,64]{1,0:T(8,128)}, u32[]{:S(2)}) copy-start(f32[16,64]{1,0:T(8,128)} %weight.1) | copy-start | bytes 12292
